TPU v7x, 32 devices: a whole 2x2x4 slice. The times are simulated.
32 devices in a mesh: sfc: 16 (over z, y, x), lev: 2 (over core).
Axes of the slice: x: 2, y: 2, z: 4, core: 2. Of those that a mesh axis runs over, the one named last changes fastest.
Arguments:
- air_state: float32 [24, 8, 32768], P(None, 'lev', 'sfc'), may hold values from -6 to 6
- metric: float32 [2, 2048], P(None, 'sfc'), may hold values from -5 to 5
- jacobian: float32 [2048], P('sfc'), may hold values from 0.25 to 4
- edge_nbr: int32 [4, 2048], P(None, 'sfc'), may hold values from 0 to 2047, as said below
- edge_side: int32 [4, 2048], P(None, 'sfc'), may hold values from 0 to 3
- coszen: float32 [32768], P('sfc'), may hold values from -1 to 1
- kappa_base: float32 [112], replicated, may hold values from 0.02 to 2
- band_kappa: float32 [112, 20], replicated, may hold values from 0.005 to 0.2
- solar_weight: float32 [112], replicated, may hold values from 0.5 to 2
- stretch_pos: int32 [32768], P('sfc'), may hold values from 0 to 32767, as said below
- stretch_src: int32 [32768], P('sfc'), may hold values from 0 to 32767, as said below
Outputs:
- new_state: float32 [24, 8, 32768], P(None, 'lev', 'sfc')
- surface_flux: float32 [32768], P(('sfc', 'lev'))
Inputs may be any that keep to these rules, and one draw needn't show every extreme that they name: edge_nbr[k, g] lies within 128 elements of g along the curve, cyclically over 2048 elements; that distance is reached. stretch_pos is a permutation of the columns and stretch_src its inverse; column c belongs to the stretch of device stretch_pos[c] // 2048; each device receives 2048 columns, at most 256 of them from one device, a bound reached in every draw; the columns that one device sends to one device take consecutive stretch positions. `stretch_src`: the inverse of stretch_pos.
All inputs are finite; a program needn't handle non-finite values.
Results may differ from a plain program's by a relative error of at most 0.0001.
Values sent between devices are 32-bit elements; how exact they have to be, the bound alone decides.
A program may use at most 64 MiB of HBM per device.

v0:
```python
import jax
import jax.numpy as jnp
import numpy as np
from jax import lax
from jax.sharding import PartitionSpec as P

NODES = 16
GBLOCK = 16


GLL_POINTS = np.array([-1.0, -1.0 / np.sqrt(5.0), 1.0 / np.sqrt(5.0), 1.0])
EDGE_NODES = np.array([[4, 8], [13, 14], [11, 7], [2, 1]], dtype=np.int32)
STEP_DYN = 0.2
DEPTH_UNIT = 0.05
HEAT_SCALE = 0.1
FLUX_SCALE = 0.02


def extended(cells, sides, width):
    for axis, dim in sides:
        count = lax.axis_size(axis)
        head = lax.slice_in_dim(cells, 0, width, axis=dim)
        tail = lax.slice_in_dim(cells, cells.shape[dim] - width, cells.shape[dim], axis=dim)
        cells = jnp.concatenate(
            [
                lax.ppermute(tail, axis, [(i, (i + 1) % count) for i in range(count)]),
                cells,
                lax.ppermute(head, axis, [((i + 1) % count, i) for i in range(count)]),
            ],
            axis=dim,
        )
    return cells


def derivative_numpy():
    spacing = GLL_POINTS[:, None] - GLL_POINTS[None, :]
    unit_diag = np.eye(4)
    safe_space = np.where(unit_diag > 0, 1.0, spacing)
    weights_row = np.prod(safe_space, axis=1)
    derivative = weights_row[:, None] / weights_row[None, :] / safe_space
    inverse_gap = np.where(unit_diag > 0, 0.0, 1.0 / safe_space)
    derivative = np.where(unit_diag > 0, inverse_gap.sum(axis=1)[:, None], derivative)
    return (np.kron(derivative, np.eye(4)), np.kron(np.eye(4), derivative))


def edge_tables():
    edge_flat = EDGE_NODES.reshape(-1)
    select_rows = np.zeros((8, 16))
    select_rows[np.arange(8), edge_flat] = 1.0
    keep_nodes = 1.0 - select_rows.sum(axis=0)
    return (select_rows, keep_nodes)


def advance(element_grid, metric, rows_i, rows_j, start):
    first_term = jnp.einsum("an,flne->flae", rows_i, element_grid, precision=lax.Precision.HIGHEST)
    second_term = jnp.einsum("an,flne->flae", rows_j, element_grid, precision=lax.Precision.HIGHEST)
    return start + STEP_DYN * (metric[0] * first_term + metric[1] * second_term)


def radiate(tracers, sun_angle, kappa_base, band_kappa, solar_weight):
    squares = tracers * tracers
    groups = kappa_base.shape[0] // GBLOCK
    level_count = tracers.shape[1]
    column_count = tracers.shape[2]

    def one_group(running, pieces):
        base_rate, rate_rows, bright = pieces
        absorb = (
            jnp.einsum("gt,tln->gln", rate_rows, squares, precision=lax.Precision.HIGHEST)
            + base_rate[:, None, None]
        )
        layer_depth = absorb * DEPTH_UNIT
        depth_above = jnp.cumsum(layer_depth, axis=1) - layer_depth
        heating = jnp.einsum(
            "g,gln->ln",
            bright,
            jnp.exp(-depth_above) * (1.0 - jnp.exp(-layer_depth)),
            precision=lax.Precision.HIGHEST,
        )
        ground = jnp.einsum(
            "g,gn->n",
            bright,
            jnp.exp(-(depth_above[:, -1] + layer_depth[:, -1])),
            precision=lax.Precision.HIGHEST,
        )
        return ((running[0] + heating, running[1] + ground), None)

    start_vals = (
        jnp.zeros((level_count, column_count), jnp.float32),
        jnp.zeros((column_count,), jnp.float32),
    )
    stacked = (
        kappa_base.reshape(groups, GBLOCK),
        band_kappa.reshape(groups, GBLOCK, -1),
        solar_weight.reshape(groups, GBLOCK),
    )
    (heating, ground), _ = lax.scan(one_group, start_vals, stacked)
    sun_height = jnp.maximum(sun_angle, 0.0)
    return (HEAT_SCALE * sun_height * heating, FLUX_SCALE * sun_height * ground)


def exchange_edges(edge_values, jacobian):
    elem_count = edge_values.shape[3]
    edge_rows = edge_values.reshape(-1, elem_count)
    edge_block = jnp.concatenate([edge_rows, jacobian[None, :]], axis=0)
    return extended(edge_block, (("sfc", 1),), elem_count)


def physics_levels(tracers, sun_angle, kappa_base, band_kappa, solar_weight):
    local_cols = tracers.shape[2]
    lev_devices = lax.axis_size("lev")
    part_cols = local_cols // lev_devices
    whole_column = lax.all_to_all(tracers, "lev", split_axis=2, concat_axis=1, tiled=True)
    sun_part = lax.dynamic_slice_in_dim(sun_angle, lax.axis_index("lev") * part_cols, part_cols)
    heating, ground = radiate(whole_column, sun_part, kappa_base, band_kappa, solar_weight)
    heat_back = lax.all_to_all(heating, "lev", split_axis=0, concat_axis=1, tiled=True)
    return (heat_back, ground)


def first_of_group(group_ids, values, group_count, sentinel):
    device_lane = jnp.arange(group_count, dtype=jnp.int32)
    member = group_ids[:, None] == device_lane[None, :]
    lowest = jnp.min(jnp.where(member, values[:, None], sentinel), axis=0)
    return values - jnp.sum(jnp.where(member, lowest[None, :], 0), axis=1)


def local(
    air_state,
    metric,
    jacobian,
    edge_nbr,
    edge_side,
    coszen,
    kappa_base,
    band_kappa,
    solar_weight,
    stretch_pos,
    stretch_src,
):
    field_count, level_count, local_cols = air_state.shape
    elem_count = local_cols // NODES
    table_i, table_j = derivative_numpy()
    select_np, keep_np = edge_tables()
    along_i = jnp.asarray(table_i, jnp.float32)
    along_j = jnp.asarray(table_j, jnp.float32)
    select_rows = jnp.asarray(select_np, jnp.float32)
    place_rows = jnp.asarray(select_np.T.copy(), jnp.float32)
    keep_nodes = jnp.asarray(keep_np, jnp.float32)
    element_grid = air_state.reshape(field_count, level_count, NODES, elem_count)
    advanced = advance(element_grid, metric, along_i, along_j, element_grid)
    edge_values = jnp.einsum(
        "an,flne->flae", select_rows, advanced, precision=lax.Precision.HIGHEST
    )
    padded = exchange_edges(edge_values, jacobian)
    sfc_devices = lax.axis_size("sfc")
    all_cols = local_cols * sfc_devices
    window_start = (lax.axis_index("sfc") - 1) * elem_count
    near_index = jnp.mod(edge_nbr - window_start, elem_count * sfc_devices)
    span_width = 3 * elem_count
    flip_pair = jnp.asarray(np.array([1, 0], dtype=np.int32))
    take_index = (2 * edge_side[:, None, :] + flip_pair[None, :, None]) * span_width + near_index[
        :, None, :
    ]
    far_rows = padded[:-1].reshape(field_count * level_count, 8 * span_width)
    far_values = jnp.take(far_rows, take_index.reshape(-1), axis=1).reshape(
        field_count, level_count, 8, elem_count
    )
    far_jac = jnp.take(padded[-1], near_index.reshape(-1)).reshape(4, 1, elem_count)
    far_jac = jnp.broadcast_to(far_jac, (4, 2, elem_count)).reshape(8, elem_count)
    summed = (jacobian * edge_values + far_jac * far_values) / (jacobian + far_jac)
    placed = jnp.einsum("ak,flke->flae", place_rows, summed, precision=lax.Precision.HIGHEST)
    dynamic = (advanced * keep_nodes[:, None] + placed).reshape(
        field_count, level_count, local_cols
    )
    capacity = 2 * local_cols // sfc_devices
    target_dev = stretch_pos // local_cols
    buffer_slot = first_of_group(target_dev, stretch_pos, sfc_devices, all_cols)
    flat_slot = target_dev * capacity + buffer_slot
    slot_column = (
        jnp.zeros((sfc_devices * capacity,), jnp.int32)
        .at[flat_slot]
        .set(jnp.arange(local_cols, dtype=jnp.int32))
    )
    source_dev = stretch_src // local_cols
    position_ids = jnp.arange(local_cols, dtype=jnp.int32)
    source_rank = first_of_group(source_dev, position_ids, sfc_devices, local_cols)
    recv_index = source_dev * capacity + source_rank
    tracer_count = field_count - 4
    tracer_rows = dynamic[4:].reshape(tracer_count * level_count, local_cols)
    sent_tracers = jnp.take(tracer_rows, slot_column, axis=1)
    sent_sun = jnp.take(coszen, slot_column)[None, :]
    got_tracers, got_sun = (
        lax.all_to_all(sent_tracers, "sfc", split_axis=1, concat_axis=1, tiled=True),
        lax.all_to_all(sent_sun, "sfc", split_axis=1, concat_axis=1, tiled=True),
    )
    stretch_tracers = jnp.take(got_tracers, recv_index, axis=1).reshape(
        tracer_count, level_count, local_cols
    )
    stretch_sun = jnp.take(got_sun[0], recv_index)
    heating, surface_flux = physics_levels(
        stretch_tracers, stretch_sun, kappa_base, band_kappa, solar_weight
    )
    position_of_slot = (
        jnp.zeros((sfc_devices * capacity,), jnp.int32).at[recv_index].set(position_ids)
    )
    returned = lax.all_to_all(
        jnp.take(heating, position_of_slot, axis=1), "sfc", split_axis=1, concat_axis=1, tiled=True
    )
    heat_cols = jnp.take(returned, flat_slot, axis=1)
    new_state = dynamic.at[2].add(heat_cols)
    return (new_state, surface_flux)


def solution(mesh):
    return jax.shard_map(
        local,
        mesh=mesh,
        in_specs=(
            P(None, "lev", "sfc"),
            P(None, "sfc"),
            P("sfc"),
            P(None, "sfc"),
            P(None, "sfc"),
            P("sfc"),
            P(),
            P(),
            P(),
            P("sfc"),
            P("sfc"),
        ),
        out_specs=(P(None, "lev", "sfc"), P(("sfc", "lev"))),
        check_vma=False,
    )
```

profile of v0, /device:TPU:0, one launch (start us, length us, event | category | flops | bytes accessed | tf_op | source)
XLA Modules:
  0.0 224.6 jit_solution(11954770912788300574)
XLA Ops:
  4.6 3.0 %collective-permute-start = (f32[769,128]{1,0:T(8,128)S(1)}, f32[769,128]{1,0:T(8,128)S(1)}, u32[]{:S(2)}, u32[]{:S(2)}) collective-permute-start(f32[769,128]{1,0:T(8,128)S(1)} %pad_maximum_fusion.3), channel_id=1, source_target_pairs={{0,2},{2,4},{4,6},{6,8},{8,10},{10,12},{12,14},{14,16},{16,18},{18... | collective-permute-start | bytes 1181192 | tf_op jit(solution)/shard_map/ppermute | solution.py:26
  7.6 4.1 %collective-permute-start.1 = (f32[769,128]{1,0:T(8,128)S(1)}, f32[769,128]{1,0:T(8,128)S(1)}, u32[]{:S(2)}, u32[]{:S(2)}) collective-permute-start(f32[769,128]{1,0:T(8,128)S(1)} %pad_maximum_fusion.3), channel_id=1, source_target_pairs={{2,0},{4,2},{6,4},{8,6},{10,8},{12,10},{14,12},{16,14},{18,16},{20... | collective-permute-start | bytes 1181192 | tf_op jit(solution)/shard_map/ppermute | solution.py:28
  12.5 8.1 %scatter_custom_fusion.1 = s32[4096]{0:T(1024)S(1)} fusion(s32[2048]{0:T(1024)S(1)} %get-tuple-element.93, s32[2048]{0:T(1024)S(1)} %iota.18, s32[]{:T(128)} %constant.211.clone.1), kind=kCustom, calls=%fused_computation.97 | custom fusion | bytes 16388 | tf_op jit(solution)/shard_map/scatter | solution.py:182
  20.6 23.0 %gather_fusion.2 = f32[4096]{0:T(1024)S(1)} fusion(f32[2048]{0:T(1024)S(1)} %copy-done, s32[4096]{0:T(1024)S(1)} %fusion.40), kind=kCustom, calls=%fused_computation.2 | custom fusion | bytes 49152 | tf_op jit(solution)/shard_map/jit(_take)/gather | solution.py:191
  44.3 3.4 %all-to-all-start = ((f32[1,16,256]{2,0,1:T(1,128)}), f32[1,16,256]{2,0,1:T(1,128)S(1)}, u32[]{:S(2)}, u32[]{:S(2)}) async-start(f32[1,16,256]{2,0,1:T(1,128)} %bitcast.24), calls=%async_computation | async-start | bytes 32768 | tf_op jit(solution)/shard_map/all_to_all | solution.py:194
  48.1 3.5 %gather_fusion = f32[512]{0:T(512)S(1)} fusion(f32[384]{0:T(512)S(1)} %maximum_reduce_fusion, s32[1024]{0:T(1024)S(1)} %pad_clamp_fusion), kind=kCustom, calls=%fused_computation | custom fusion | bytes 6144 | tf_op jit(solution)/shard_map/jit(_take)/gather | solution.py:168
  61.3 10.8 %gather_fusion.4 = f32[4096,80]{1,0:T(8,128)S(1)} fusion(f32[80,2048]{0,1:T(8,128)S(1)} %copy.80, s32[4096]{0:T(1024)S(1)} %fusion.40), kind=kCustom, calls=%fused_computation.4 | custom fusion | bytes 2637824 | tf_op jit(solution)/shard_map/jit(_take)/gather | solution.py:190
  76.4 7.0 %all-to-all-start.1 = ((f32[80,16,256]{2,0,1:T(8,128)}), f32[80,16,256]{2,0,1:T(8,128)S(1)}, u32[]{:S(2)}, u32[]{:S(2)}) async-start(f32[80,16,256]{2,0,1:T(8,128)} %broadcast_select_fusion), calls=%async_computation.1 | async-start | bytes 2621440 | tf_op jit(solution)/shard_map/all_to_all | solution.py:193
  85.1 8.2 %scatter_custom_fusion = s32[4096]{0:T(1024)S(1)} fusion(s32[2048]{0:T(1024)S(1)} %get-tuple-element.97, s32[2048]{0:T(1024)S(1)} %iota.17, s32[]{:T(128)} %constant.211.clone.1), kind=kCustom, calls=%fused_computation.99 | custom fusion | bytes 16388 | tf_op jit(solution)/shard_map/scatter | solution.py:204
  94.0 11.8 %gather_fusion.3 = f32[2048]{0:T(1024)S(1)} fusion(f32[4096]{0:T(1024)S(1)} %bitcast.132, s32[2048]{0:T(1024)S(1)} %broadcast_clamp_fusion.1), kind=kCustom, calls=%fused_computation.3 | custom fusion | bytes 24576 | tf_op jit(solution)/shard_map/jit(_take)/gather | solution.py:199
  105.8 6.5 %all-to-all-done.1 = f32[80,16,256]{2,0,1:T(8,128)S(1)} async-done(((f32[80,16,256]{2,0,1:T(8,128)}), f32[80,16,256]{2,0,1:T(8,128)S(1)}, u32[]{:S(2)}, u32[]{:S(2)}) %all-to-all-start.1) | async-done | bytes 1310752 | tf_op jit(solution)/shard_map/all_to_all | solution.py:193
  113.1 5.5 %gather_fusion.5 = f32[2048,80]{1,0:T(8,128)S(1)} fusion(f32[80,4096]{0,1:T(8,128)S(1)} %bitcast.134, s32[2048]{0:T(1024)S(1)} %broadcast_clamp_fusion.1), kind=kCustom, calls=%fused_computation.5 | custom fusion | bytes 1318912 | tf_op jit(solution)/shard_map/jit(_take)/gather | solution.py:196
  119.5 3.2 %copy.84 = f32[20,4,2048]{0,1,2:T(4,128)} copy(f32[20,4,2048]{2,1,0:T(4,128)S(1)} %broadcast_select_fusion.1) | data formatting | bytes 1310720 | tf_op jit(solution)/shard_map/jit(_take)/select_n | solution.py:196
  122.6 7.2 %reshape.428 = f32[2,1,81920]{2,1,0:T(1,128)S(1)} reshape(f32[2048,4,20]{2,1,0:T(4,128)} %bitcast.135) | data formatting | bytes 1310720
  129.9 4.3 %all_to_all.52 = f32[2,1,81920]{2,1,0:T(1,128)S(1)} all-to-all(f32[2,1,81920]{2,1,0:T(1,128)S(1)} %reshape.428), channel_id=1, replica_groups=mesh['sfc'=16,'lev'=2] {'lev'}, dimensions={0} | all-to-all | bytes 1310720 | tf_op jit(solution)/shard_map/all_to_all | solution.py:113
  137.3 8.0 %reshape.429 = f32[2048,4,20]{2,1,0:T(4,128)} reshape(f32[2,81920]{1,0:T(2,128)S(1)} %reduce.4) | data formatting | bytes 1310720
  145.3 3.9 %bitcast_multiply_fusion.1 = f32[20,4,2048]{0,1,2:T(4,128)} fusion(f32[2048,4,20]{2,1,0:T(4,128)} %reshape.429), kind=kLoop, calls=%fused_computation.129 | loop fusion | flops 163840 | bytes 1310720 | tf_op jit(solution)/shard_map/mul | solution.py:61
  149.2 3.5 %copy.85 = f32[20,2,4,1024]{3,0,2,1:T(8,128)S(1)} copy(f32[20,2,4,1024]{0,2,3,1:T(4,128)} %bitcast.136) | data formatting | bytes 1310720 | tf_op jit(solution)/shard_map/mul | solution.py:61
  152.7 29.1 %while.14 = (s32[]{:T(128)}, f32[8,1024]{1,0:T(8,128)S(1)}, f32[1024]{0:T(1024)S(1)}, f32[7,16]{1,0:T(8,128)S(1)}, f32[7,16,20]{2,1,0:T(8,128)S(1)}, /*index=5*/...) while((s32[]{:T(128)}, f32[8,1024]{1,0:T(8,128)S(1)}, f32[1024]{0:T(1024)S(1)}, ...), condition=%wide.region_8.9_spmd.clone, body=%wide.region_6.8_spmd.clone.sunk | while | flops 35112960 | bytes 3696376 | solution.py:97
  182.4 3.7 %all_to_all.53 = f32[2,4,1024]{2,1,0:T(4,128)S(1)} all-to-all(f32[2,4,1024]{2,1,0:T(4,128)S(1)} %all_to_all.41), channel_id=1, replica_groups=mesh['sfc'=16,'lev'=2] {'lev'}, dimensions={0} | all-to-all | bytes 65536 | tf_op jit(solution)/shard_map/all_to_all | solution.py:116
  186.6 14.1 %gather_fusion.6 = f32[4096,4]{1,0:T(8,128)} fusion(f32[4,2048]{0,1:T(8,128)S(1)} %bitcast.145, s32[4096]{0:T(1024)S(1)} %fusion.39), kind=kCustom, calls=%fused_computation.6 | custom fusion | bytes 147456 | tf_op jit(solution)/shard_map/jit(_take)/gather | solution.py:207
  203.6 6.4 %all-to-all-start.4 = ((f32[4,16,256]{2,0,1:T(4,128)}), f32[4,16,256]{2,0,1:T(4,128)S(1)}, u32[]{:S(2)}, u32[]{:S(2)}) async-start(f32[4,16,256]{2,0,1:T(4,128)} %broadcast_select_fusion.2), calls=%async_computation.4 | async-start | bytes 131072 | tf_op jit(solution)/shard_map/all_to_all | solution.py:206
  211.1 6.3 %all-to-all-done.4 = f32[4,16,256]{2,0,1:T(4,128)S(1)} async-done(((f32[4,16,256]{2,0,1:T(4,128)}), f32[4,16,256]{2,0,1:T(4,128)S(1)}, u32[]{:S(2)}, u32[]{:S(2)}) %all-to-all-start.4) | async-done | bytes 65568 | tf_op jit(solution)/shard_map/all_to_all | solution.py:206
  218.1 5.5 %gather_fusion.7 = f32[2048,4]{1,0:T(8,128)S(1)} fusion(f32[4,4096]{0,1:T(8,128)S(1)} %bitcast.142, s32[2048]{0:T(1024)S(1)} %broadcast_clamp_fusion), kind=kCustom, calls=%fused_computation.7 | custom fusion | bytes 73728 | tf_op jit(solution)/shard_map/jit(_take)/gather | solution.py:209
  (172 shorter events, 61.8 us)
Async XLA Ops:
  0.6 19.9 %copy-start = (f32[2048]{0:T(1024)S(1)}, f32[2048]{0:T(1024)}, u32[]{:S(2)}) copy-start(f32[2048]{0:T(1024)} %param.26) | copy-start | bytes 24580
  0.6 1.6 copy-start.10
  0.7 2.4 %copy-start.13 = (f32[16,16,1,1]{1,0,3,2:T(8,128)S(1)}, f32[16,16,1,1]{1,0,3,2:T(8,128)}, u32[]{:S(2)}) copy-start(f32[16,16,1,1]{1,0,3,2:T(8,128)} %constant.237) | copy-start | bytes 3076
  0.7 1.6 copy-start.18
  3.1 0.9 copy-start.15
  3.1 1.4 copy-start.8
  4.0 7.7 %copy-start.4 = (s32[2048]{0:T(1024)S(1)}, s32[2048]{0:T(1024)}, u32[]{:S(2)}) copy-start(s32[2048]{0:T(1024)} %param.30) | copy-start | bytes 24580
  4.6 43.5 %collective-permute-start = (f32[769,128]{1,0:T(8,128)S(1)}, f32[769,128]{1,0:T(8,128)S(1)}, u32[]{:S(2)}, u32[]{:S(2)}) collective-permute-start(f32[769,128]{1,0:T(8,128)S(1)} %pad_maximum_fusion.3), channel_id=1, source_target_pairs={{0,2},{2,4},{4,6},{6,8},{8,10},{10,12},{12,14},{14,16},{16,18},{18... | collective-permute-start | bytes 1181192 | tf_op jit(solution)/shard_map/ppermute | solution.py:26
  7.6 40.5 %collective-permute-start.1 = (f32[769,128]{1,0:T(8,128)S(1)}, f32[769,128]{1,0:T(8,128)S(1)}, u32[]{:S(2)}, u32[]{:S(2)}) collective-permute-start(f32[769,128]{1,0:T(8,128)S(1)} %pad_maximum_fusion.3), channel_id=1, source_target_pairs={{2,0},{4,2},{6,4},{8,6},{10,8},{12,10},{14,12},{16,14},{18,16},{20... | collective-permute-start | bytes 1181192 | tf_op jit(solution)/shard_map/ppermute | solution.py:28
  20.6 27.1 %copy-start.11 = (s32[4,128]{1,0:T(4,128)S(1)}, s32[4,128]{1,0:T(4,128)}, u32[]{:S(2)}) copy-start(s32[4,128]{1,0:T(4,128)} %param.24) | copy-start | bytes 6148
  20.6 27.2 %copy-start.17 = (s32[4,128]{1,0:T(4,128)S(1)}, s32[4,128]{1,0:T(4,128)}, u32[]{:S(2)}) copy-start(s32[4,128]{1,0:T(4,128)} %param.25) | copy-start | bytes 6148
  20.6 27.2 %copy-start.16 = (s32[2]{0:T(128)S(1)}, s32[2]{0:T(128)}, u32[]{:S(2)}) copy-start(s32[2]{0:T(128)} %constant.236.clone) | copy-start | bytes 28
  44.3 32.1 %all-to-all-start = ((f32[1,16,256]{2,0,1:T(1,128)}), f32[1,16,256]{2,0,1:T(1,128)S(1)}, u32[]{:S(2)}, u32[]{:S(2)}) async-start(f32[1,16,256]{2,0,1:T(1,128)} %bitcast.24), calls=%async_computation | async-start | bytes 32768 | tf_op jit(solution)/shard_map/all_to_all | solution.py:194
  48.1 3.5 %copy-start.3 = (f32[769,128]{1,0:T(8,128)}, f32[769,128]{1,0:T(8,128)S(1)}, u32[]{:S(2)}) copy-start(f32[769,128]{1,0:T(8,128)S(1)} %collective-permute-done.1) | copy-start | bytes 1181188
  76.3 7.1 %copy-start.9 = (f32[112,20]{0,1:T(8,128)S(1)}, f32[112,20]{0,1:T(8,128)}, u32[]{:S(2)}) copy-start(f32[112,20]{0,1:T(8,128)} %param.28) | copy-start | bytes 26884
  76.3 7.2 %copy-start.19 = (f32[112]{0:T(128)S(1)}, f32[112]{0:T(128)}, u32[]{:S(2)}) copy-start(f32[112]{0:T(128)} %param.29) | copy-start | bytes 1348
  76.3 7.3 %copy-start.20 = (f32[112]{0:T(128)S(1)}, f32[112]{0:T(128)}, u32[]{:S(2)}) copy-start(f32[112]{0:T(128)} %param.27) | copy-start | bytes 1348
  76.3 7.9 %copy-start.5 = (s32[2048]{0:T(1024)S(1)}, s32[2048]{0:T(1024)}, u32[]{:S(2)}) copy-start(s32[2048]{0:T(1024)} %param.31) | copy-start | bytes 24580
  76.4 36.0 %all-to-all-start.1 = ((f32[80,16,256]{2,0,1:T(8,128)}), f32[80,16,256]{2,0,1:T(8,128)S(1)}, u32[]{:S(2)}, u32[]{:S(2)}) async-start(f32[80,16,256]{2,0,1:T(8,128)} %broadcast_select_fusion), calls=%async_computation.1 | async-start | bytes 2621440 | tf_op jit(solution)/shard_map/all_to_all | solution.py:193
  186.5 16.3 %copy-start.6 = (pred[16,256]{1,0:T(8,128)(4,1)S(1)}, pred[16,256]{1,0:T(8,128)(4,1)}, u32[]{:S(2)}) copy-start(pred[16,256]{1,0:T(8,128)(4,1)} %broadcast_in_dim.162) | copy-start | bytes 12292
  186.6 23.4 %copy-start.2 = (f32[24,4,16,128]{3,2,1,0:T(8,128)S(1)}, f32[24,4,16,128]{3,2,1,0:T(8,128)}, u32[]{:S(2)}) copy-start(f32[24,4,16,128]{3,2,1,0:T(8,128)} %copy-done.1) | copy-start | bytes 2359300
  200.7 10.4 %slice-start = ((f32[24,4,16,128]{3,2,1,0:T(8,128)}), f32[1,4,16,128]{3,2,1,0:T(8,128)S(1)}, s32[]{:S(2)}) async-start(f32[24,4,16,128]{3,2,1,0:T(8,128)} %copy-done.1), calls=%async_computation.5 | async-start | bytes 65536 | tf_op jit(solution)/shard_map/slice.28
  203.6 13.9 %all-to-all-start.4 = ((f32[4,16,256]{2,0,1:T(4,128)}), f32[4,16,256]{2,0,1:T(4,128)S(1)}, u32[]{:S(2)}, u32[]{:S(2)}) async-start(f32[4,16,256]{2,0,1:T(4,128)} %broadcast_select_fusion.2), calls=%async_computation.4 | async-start | bytes 131072 | tf_op jit(solution)/shard_map/all_to_all | solution.py:206
  211.1 12.8 %copy-start.12 = (pred[2048]{0:T(1024)(128)(4,1)S(1)}, pred[2048]{0:T(1024)(128)(4,1)}, u32[]{:S(2)}) copy-start(pred[2048]{0:T(1024)(128)(4,1)} %get-tuple-element.92) | copy-start | bytes 6148
  (4 other events, 2.9 us)
where the time goes:
time: 226 us; the launch traced here: 225 us
  local copies, waits for them, and re-layouts  136 us (60%)
  other arithmetic  30 us (13%)
  starting transfers between devices  23.9 us (11%)
  waiting for transfers between devices  12.9 us (6%)
  matrix products  11.6 us (5%)
  blocking collectives  8.01 us (4%)
    gather x1, local copies, waits for them, and re-layouts, local(): sent_sun = jnp.take(coszen, slot_column)[None, :]  23 us
    unnamed x49, local copies, waits for them, and re-layouts  16.8 us
    gather x2, local copies, waits for them, and re-layouts, local(): jnp.take(heating, position_of_slot, axis=1)  16.3 us
    another operation x7, other arithmetic, one_group(): depth_above = jnp.cumsum(layer_depth, axis=1) - layer_depth  15 us
    gather x2, local copies, waits for them, and re-layouts, local(): sent_tracers = jnp.take(tracer_rows, slot_column, axis=1)  12.5 us
    gather x1, local copies, waits for them, and re-layouts, local(): stretch_sun = jnp.take(got_sun[0], recv_index)  11.8 us
    scatter x1, local copies, waits for them, and re-layouts, local(): jnp.zeros((sfc_devices * capacity,), jnp.int32).at[recv_index]  8.24 us
    scatter x1, local copies, waits for them, and re-layouts, local(): slot_column = jnp.zeros((sfc_devices * capacity,), jnp.int32).at[flat_slo...  8.06 us
  transfers between devices with their start and end apart: 5, of which 2 were waited for; matrix products, arithmetic and copies ran while one was open for 37% of the time, Pallas kernels for 0%

commit v1 on v0

v1 whole, which is shorter than its diff:
```python
import functools

import jax
import jax.numpy as jnp
import numpy as np
from jax import lax
from jax.experimental import pallas as pl
from jax.experimental.pallas import tpu as pltpu
from jax.sharding import PartitionSpec as P

NODES = 16
GLL_POINTS = np.array([-1.0, -1.0 / np.sqrt(5.0), 1.0 / np.sqrt(5.0), 1.0])
EDGE_NODES = ((4, 8), (13, 14), (11, 7), (2, 1))
STEP_DYN = 0.2
DEPTH_UNIT = 0.05
HEAT_SCALE = 0.1
FLUX_SCALE = 0.02
F32 = jnp.float32
BF16 = jnp.bfloat16


def derivative_matrix():
    spacing = GLL_POINTS[:, None] - GLL_POINTS[None, :]
    unit_diag = np.eye(4)
    safe_space = np.where(unit_diag > 0, 1.0, spacing)
    weights_row = np.prod(safe_space, axis=1)
    derivative = weights_row[:, None] / weights_row[None, :] / safe_space
    inverse_gap = np.where(unit_diag > 0, 0.0, 1.0 / safe_space)
    return np.where(unit_diag > 0, inverse_gap.sum(axis=1)[:, None], derivative)


def split2(x):
    high = x.astype(BF16)
    return high, (x - high.astype(F32)).astype(BF16)


def dot(a, b):
    return jnp.dot(a, b, preferred_element_type=F32)


def advance_kernel(x_ref, metric_ref, adv_ref, edge_ref):
    rows, cols = x_ref.shape
    ne = cols // NODES
    d = derivative_matrix()
    m0 = jnp.broadcast_to(STEP_DYN * metric_ref[0:1, :], (8, ne))
    m1 = jnp.broadcast_to(STEP_DYN * metric_ref[1:2, :], (8, ne))

    def step(r, carry):
        sl = pl.ds(pl.multiple_of(r * 8, 8), 8)
        x = [x_ref[sl, n * ne : (n + 1) * ne] for n in range(NODES)]
        out = []
        for i in range(4):
            for j in range(4):
                first = sum(float(d[i, a]) * x[4 * a + j] for a in range(4))
                second = sum(float(d[j, a]) * x[4 * i + a] for a in range(4))
                out.append(x[4 * i + j] + (m0 * first + m1 * second))
        for n in range(NODES):
            adv_ref[sl, n * ne : (n + 1) * ne] = out[n]
        low = pl.ds(pl.multiple_of(rows + r * 8, 8), 8)
        for k, (a, b) in enumerate(EDGE_NODES):
            edge_ref[sl, k * ne : (k + 1) * ne] = out[b]
            edge_ref[low, k * ne : (k + 1) * ne] = out[a]
        return carry

    lax.fori_loop(0, rows // 8, step, 0)


def edge_kernel(
    levels, adv_ref, own_ref, left_ref, right_ref, jac_ref, target_ref, dyn_ref, sq_ref
):
    rows, cols = adv_ref.shape
    ne = cols // NODES
    fields = rows // levels
    width = 4 * ne
    target = target_ref[...]
    acc = jnp.zeros((2 * rows + 16, width), F32)
    for w, ref in enumerate((left_ref, own_ref, right_ref)):
        lanes = lax.broadcasted_iota(jnp.int32, (width, width), 0) + w * width
        onehot = jnp.where(lanes == target, 1.0, 0.0).astype(BF16)
        jac = jnp.concatenate([jac_ref[w : w + 1, :]] * 4, axis=1)
        src = jnp.concatenate([ref[...], jnp.broadcast_to(jac, (16, width))], axis=0)
        high, low = split2(src)
        acc = acc + dot(high, onehot) + dot(low, onehot)
    own_jac = jnp.concatenate([jac_ref[1:2, :]] * 4, axis=1)
    far_jac = acc[2 * rows : 2 * rows + 1, :]
    total = own_jac + far_jac
    own_part, far_part = own_jac / total, far_jac / total
    first = own_part * own_ref[rows:, :] + far_part * acc[:rows]
    second = own_part * own_ref[:rows, :] + far_part * acc[rows : 2 * rows]
    where = {}
    for k, (a, b) in enumerate(EDGE_NODES):
        where[a], where[b] = (first, k), (second, k)
    for n in range(NODES):
        sl = slice(n * ne, (n + 1) * ne)
        if n in where:
            values, k = where[n]
            piece = values[:, k * ne : (k + 1) * ne]
        else:
            piece = adv_ref[:, sl]
        dyn_ref[:, sl] = piece
        squares = piece * piece
        sq_ref[:, sl] = sum(squares[l * fields : (l + 1) * fields] for l in range(levels))


def physics_kernel(
    levels, top_ref, dyn_ref, own_ref, other_ref, rate_ref, base_ref, weight_ref, sun_ref, out_ref, flux_ref
):
    fields = dyn_ref.shape[0] // levels
    top = top_ref[0]
    rates, base, weight = rate_ref[...], base_ref[...], weight_ref[...]
    other = other_ref[...]

    def light(sums, count):
        high = sums.astype(BF16).astype(F32)
        stacked = jnp.concatenate([high, sums - high, high], axis=0).astype(BF16)
        depth = dot(rates, stacked) + count * base
        return jnp.sum(weight * jnp.exp(depth), axis=0, keepdims=True)

    sun = jnp.maximum(sun_ref[...], 0.0)
    extra = light(other + top * own_ref[...], levels * (1.0 + top))
    above = top * jnp.sum(weight) + (1.0 - top) * extra
    running = (1.0 - top) * other
    out_ref[...] = dyn_ref[...]
    for l in range(levels):
        part = dyn_ref[l * fields : (l + 1) * fields, :]
        running = running + part * part
        below = light(running, (1.0 - top) * levels + (l + 1.0))
        row = l * fields + 2
        out_ref[row : row + 1, :] = dyn_ref[row : row + 1, :] + HEAT_SCALE * sun * (above - below)
        above = below
    flux_ref[...] = FLUX_SCALE * sun * (top * extra + (1.0 - top) * above)


def lookup_kernel(table_ref, index_ref, out_ref):
    rows = table_ref.shape[0]
    count = index_ref.shape[1]
    index = index_ref[...]
    high_index, lane_index = index >> 7, index & 127
    onehot = jnp.where(
        lax.broadcasted_iota(jnp.int32, (rows, count), 0) == high_index, 1.0, 0.0
    ).astype(BF16)
    table = table_ref[...].T
    high, rest = split2(table)
    low, tail = split2(table - high.astype(F32))
    picked = dot(high, onehot) + dot(low, onehot) + dot(tail, onehot)
    mask = lax.broadcasted_iota(jnp.int32, (128, count), 0) == lane_index
    out_ref[...] = jnp.sum(jnp.where(mask, picked, 0.0), axis=0, keepdims=True)


def local(
    air_state,
    metric,
    jacobian,
    edge_nbr,
    edge_side,
    coszen,
    kappa_base,
    band_kappa,
    solar_weight,
    stretch_pos,
    stretch_src,
):
    fields, levels, cols = air_state.shape
    ne = cols // NODES
    rows = fields * levels
    count = lax.axis_size("sfc")
    forward = [(i, (i + 1) % count) for i in range(count)]
    backward = [((i + 1) % count, i) for i in range(count)]
    sds = jax.ShapeDtypeStruct

    state = air_state.transpose(1, 0, 2).reshape(rows, cols)
    jac = jacobian[None, :]
    jac3 = jnp.concatenate(
        [lax.ppermute(jac, "sfc", forward), jac, lax.ppermute(jac, "sfc", backward)], axis=0
    )
    near = jnp.mod(edge_nbr - (lax.axis_index("sfc") - 1) * ne, ne * count)
    target = (near // ne) * (4 * ne) + edge_side * ne + near % ne

    advanced, edges = pl.pallas_call(
        advance_kernel,
        out_shape=(sds((rows, cols), F32), sds((2 * rows, 4 * ne), F32)),
        name="advance",
    )(state, metric)
    left = lax.ppermute(edges, "sfc", forward)
    right = lax.ppermute(edges, "sfc", backward)
    dynamic, squares = pl.pallas_call(
        functools.partial(edge_kernel, levels),
        out_shape=(sds((rows, cols), F32), sds((fields, cols), F32)),
        name="edges",
    )(advanced, edges, left, right, jac3, target.reshape(1, 4 * ne))
    other = lax.ppermute(squares, "lev", [(0, 1), (1, 0)])

    rates = jnp.pad(-DEPTH_UNIT * band_kappa, ((0, 0), (fields - band_kappa.shape[1], 0)))
    high = lax.reduce_precision(rates, 8, 7)
    low = lax.reduce_precision(rates - high, 8, 7)
    stacked_rates = jnp.concatenate([high, high, low], axis=1).astype(BF16)
    points = kappa_base.shape[0]
    top = (lax.axis_index("lev") == 0).astype(F32).reshape(1)
    chunk = min(cols, 512)
    whole = lambda shape: pl.BlockSpec(shape, lambda i: (0, 0))
    block = lambda height: pl.BlockSpec((height, chunk), lambda i: (0, i))
    updated, flux = pl.pallas_call(
        functools.partial(physics_kernel, levels),
        grid=(cols // chunk,),
        in_specs=[
            pl.BlockSpec(memory_space=pltpu.SMEM),
            block(rows),
            block(fields),
            block(fields),
            whole((points, 3 * fields)),
            whole((points, 1)),
            whole((points, 1)),
            block(1),
        ],
        out_specs=(block(rows), block(1)),
        out_shape=(sds((rows, cols), F32), sds((1, cols), F32)),
        name="physics",
    )(
        top,
        dynamic,
        squares,
        other,
        stacked_rates,
        -DEPTH_UNIT * kappa_base[:, None],
        solar_weight[:, None],
        coszen[None, :],
    )
    new_state = updated.reshape(levels, fields, cols).transpose(1, 0, 2)

    table = lax.all_to_all(
        jnp.broadcast_to(flux.reshape(1, cols // 128, 128), (count, cols // 128, 128)),
        "sfc",
        split_axis=0,
        concat_axis=0,
        tiled=True,
    ).reshape(count * cols // 128, 128)
    part = cols // lax.axis_size("lev")
    index = lax.dynamic_slice_in_dim(stretch_src, lax.axis_index("lev") * part, part)
    surface_flux = pl.pallas_call(
        lookup_kernel, out_shape=sds((1, part), F32), name="lookup"
    )(table, index[None, :])
    return (new_state, surface_flux.reshape(part))


def solution(mesh):
    return jax.shard_map(
        local,
        mesh=mesh,
        in_specs=(
            P(None, "lev", "sfc"),
            P(None, "sfc"),
            P("sfc"),
            P(None, "sfc"),
            P(None, "sfc"),
            P("sfc"),
            P(),
            P(),
            P(),
            P("sfc"),
            P("sfc"),
        ),
        out_specs=(P(None, "lev", "sfc"), P(("sfc", "lev"))),
        check_vma=False,
    )
```

time: 226 us -> 60.7 us (0.27)
  local copies, waits for them, and re-layouts: 136 us -> 12.6 us
  other arithmetic: 30 us -> 1.98 us
  Pallas kernels: 0 us -> 12.3 us
  matrix products: 11.6 us -> 0 us
  blocking collectives: 8.01 us -> 0 us
  starting transfers between devices: 23.9 us -> 19.4 us
    gather x14 -> x0, local copies, waits for them, and re-layouts: 81.9 us -> none  [the longest x1 23 us: local(): sent_sun = jnp.take(coszen, slot_column)[None, :]]
    scatter x2 -> x0, local copies, waits for them, and re-layouts: 16.3 us -> none  [the longest x1 8.24 us: local(): jnp.zeros((sfc_devices * capacity,), jnp.int32).at[recv_index]]
    another operation x7 -> x1, other arithmetic: 15 us -> 0.08 us  [one_group(): depth_above = jnp.cumsum(layer_depth, axis=1) - layer_depth]
    unnamed x49 -> x23, local copies, waits for them, and re-layouts: 16.8 us -> 4.22 us
    pallas_call x0 -> x4, Pallas kernels: none -> 12.3 us  [the longest x1 4.22 us: local(): pl.pallas_call(functools.partial(physics_kernel, levels), grid=(cols // c...]
    dot_general x25 -> x0, matrix products: 11.6 us -> none  [the longest x7 4.01 us: one_group(): jnp.einsum('gt,tln->gln', rate_rows, squares, precision=lax.Precision.HIG...]
    all_to_all x3 -> x1, starting transfers between devices: 16.8 us -> 6.85 us  [local(): lax.all_to_all(jnp.broadcast_to(flux.reshape(1, cols // 128, 128), (count...]
    ppermute x2 -> x5, waiting for transfers between devices: 0.01 us -> 8.38 us  [the longest x1 7.31 us: local(): left = lax.ppermute(edges, 'sfc', forward)]
  transfers between devices with their start and end apart: 5 -> 6, of which waited for: 2 -> 4; matrix products, arithmetic and copies ran while one was open for 37% -> 15% of each run, Pallas kernels for 0% -> 4%
where the time goes in v1:
time: 60.7 us; the launch traced here: 60.1 us
  starting transfers between devices  19.4 us (32%)
  waiting for transfers between devices  13.1 us (22%)
  local copies, waits for them, and re-layouts  12.6 us (21%)
  Pallas kernels  12.3 us (20%)
  other arithmetic  1.98 us (3%)
  between operations  0.71 us (1%)
    ppermute x1, waiting for transfers between devices, local(): left = lax.ppermute(edges, 'sfc', forward)  7.31 us
    all_to_all x1, starting transfers between devices, local(): lax.all_to_all(jnp.broadcast_to(flux.reshape(1, cols // 128, 128), (count...  6.85 us
    ppermute x1, starting transfers between devices, local(): right = lax.ppermute(edges, 'sfc', backward)  5.62 us
    all_to_all x1, waiting for transfers between devices, local(): lax.all_to_all(jnp.broadcast_to(flux.reshape(1, cols // 128, 128), (count...  4.67 us
    unnamed x23, local copies, waits for them, and re-layouts  4.22 us
    pallas_call x1, Pallas kernels, local(): pl.pallas_call(functools.partial(physics_kernel, levels), grid=(cols // c...  4.22 us
    ppermute x1, starting transfers between devices, local(): lax.ppermute(jac, 'sfc', backward)  4 us
    pallas_call x1, Pallas kernels, local(): pl.pallas_call(functools.partial(edge_kernel, levels), out_shape=(sds((ro...  3.43 us
  transfers between devices with their start and end apart: 6, of which 4 were waited for; matrix products, arithmetic and copies ran while one was open for 15% of the time, Pallas kernels for 4%

profile of v1, /device:TPU:0, one launch (start us, length us, event | category | flops | bytes accessed | tf_op | source)
XLA Modules:
  0.0 60.1 jit_solution(17478240072971422407)
XLA Ops:
  0.6 0.6 %copy-done.9 = f32[128]{0:T(128)S(1)} copy-done((f32[128]{0:T(128)S(1)}, f32[128]{0:T(128)}, u32[]{:S(2)}) %copy-start.9) | copy-done | bytes 536
  1.3 3.0 %collective-permute-start.2 = (f32[1,128]{1,0:T(1,128)S(1)}, f32[1,128]{1,0:T(1,128)S(1)}, u32[]{:S(2)}, u32[]{:S(2)}) collective-permute-start(f32[1,128]{1,0:T(1,128)S(1)} %bitcast.28), channel_id=1, source_target_pairs={{0,2},{2,4},{4,6},{6,8},{8,10},{10,12},{12,14},{14,16},{16,18},{18... | collective-permute-start | bytes 1544 | tf_op jit(solution)/shard_map/ppermute | solution.py:174
  4.3 4.0 %collective-permute-start.3 = (f32[1,128]{1,0:T(1,128)S(1)}, f32[1,128]{1,0:T(1,128)S(1)}, u32[]{:S(2)}, u32[]{:S(2)}) collective-permute-start(f32[1,128]{1,0:T(1,128)S(1)} %bitcast.29), channel_id=1, source_target_pairs={{2,0},{4,2},{6,4},{8,6},{10,8},{12,10},{14,12},{16,14},{18,16},{20... | collective-permute-start | bytes 1544 | tf_op jit(solution)/shard_map/ppermute | solution.py:174
  8.2 2.5 %copy.17 = f32[4,24,2048]{2,1,0:T(8,128)} copy(f32[4,24,2048]{2,0,1:T(4,128)} %bitcast.18) | data formatting | bytes 1572864 | tf_op jit(solution)/shard_map/transpose | solution.py:171
  10.7 2.7 %advance.1 = (f32[96,2048]{1,0:T(8,128)}, f32[192,512]{1,0:T(8,128)}) custom-call(f32[96,2048]{1,0:T(8,128)} %bitcast.17, f32[2,128]{1,0:T(2,128)} %metric_ref.1), custom_call_target="tpu_custom_call" | custom-call | tf_op jit(solution)/shard_map/advance/pallas_call | solution.py:179
  13.4 5.6 %collective-permute-start.1 = (f32[192,512]{1,0:T(8,128)}, f32[192,512]{1,0:T(8,128)S(1)}, u32[]{:S(2)}, u32[]{:S(2)}) collective-permute-start(f32[192,512]{1,0:T(8,128)} %get-tuple-element.9.own_ref), channel_id=1, source_target_pairs={{2,0},{4,2},{6,4},{8,6},{10,8},{12,10},{14,12},{16,14},{18,16},{20... | collective-permute-start | bytes 1179656 | tf_op jit(solution)/shard_map/ppermute | solution.py:185
  19.2 0.6 %copy-done.7 = s32[4,128]{1,0:T(4,128)S(1)} copy-done((s32[4,128]{1,0:T(4,128)S(1)}, s32[4,128]{1,0:T(4,128)}, u32[]{:S(2)}) %copy-start.7) | copy-done | bytes 2072
  19.9 0.6 %fusion.5 = s32[4,128]{1,0:T(4,128)} fusion(s32[4,128]{1,0:T(4,128)S(1)} %copy-done.6, s32[4,128]{1,0:T(4,128)S(1)} %copy-done.7, s32[]{:T(128)S(6)} %mul.30), kind=kLoop, calls=%fused_computation.18 | loop fusion | flops 17920 | bytes 6148 | tf_op jit(solution)/shard_map/add | solution.py:177
  20.5 0.7 %copy.20.base_ref = f32[112,1]{1,0:T(8,128)} copy(f32[112,1]{0,1:T(1,128)S(1)} %multiply_bitcast_fusion) | data formatting | bytes 896 | tf_op jit(solution)/shard_map/mul | solution.py:224
  21.3 0.7 %copy-done.8 = f32[112]{0:T(128)S(1)} copy-done((f32[112]{0:T(128)S(1)}, f32[112]{0:T(128)}, u32[]{:S(2)}) %copy-start.8) | copy-done | bytes 472
  21.9 0.7 %copy.21.weight_ref = f32[112,1]{1,0:T(8,128)} copy(f32[112,1]{0,1:T(1,128)S(1)} %bitcast.27) | data formatting | bytes 896 | tf_op jit(solution)/shard_map/broadcast_in_dim | solution.py:225
  23.2 7.3 %collective-permute-done.left_ref = f32[192,512]{1,0:T(8,128)S(1)} collective-permute-done((f32[192,512]{1,0:T(8,128)}, f32[192,512]{1,0:T(8,128)S(1)}, u32[]{:S(2)}, u32[]{:S(2)}) %collective-permute-start) | collective-permute-done | bytes 393248 | tf_op jit(solution)/shard_map/ppermute | solution.py:184
  31.5 3.4 %edges.1 = (f32[96,2048]{1,0:T(8,128)}, f32[24,2048]{1,0:T(8,128)}) custom-call(f32[96,2048]{1,0:T(8,128)} %get-tuple-element.8.adv_ref, f32[192,512]{1,0:T(8,128)} %get-tuple-element.9.own_ref, f32[192,512]{1,0:T(8,128)} %copy-done.1, f32[192,512]{1,0:T(8,128)} %copy-done.2, f32[3,128]{1,0:T(4,128)} %pad_maximum_fusion.1.jac_ref, s32[1,512]{1,0:T(1,128)} %bitcast.25), custom_call_target="tpu_custom_call" | custom-call | tf_op jit(solution)/shard_map/edges/pallas_call | solution.py:186
  35.0 0.7 %pad_maximum_fusion.rate_ref = bf16[112,72]{1,0:T(8,128)(2,1)} fusion(bf16[112,24]{1,0:T(8,128)(2,1)S(1)} %get-tuple-element.15, bf16[112,24]{1,0:T(8,128)(2,1)S(1)} %get-tuple-element.14), kind=kLoop, calls=%fused_computation.5 | loop fusion | flops 48384 | bytes 26880 | tf_op jit(solution)/shard_map/concatenate | solution.py:196
  35.7 0.9 %collective-permute-done.4.other_ref = f32[24,2048]{1,0:T(8,128)S(1)} collective-permute-done((f32[24,2048]{1,0:T(8,128)}, f32[24,2048]{1,0:T(8,128)S(1)}, u32[]{:S(2)}, u32[]{:S(2)}) %collective-permute-start.4) | collective-permute-done | bytes 196640 | tf_op jit(solution)/shard_map/ppermute | solution.py:191
  36.6 0.7 %copy-done.3 = f32[24,2048]{1,0:T(8,128)} copy-done((f32[24,2048]{1,0:T(8,128)}, f32[24,2048]{1,0:T(8,128)S(1)}, u32[]{:S(2)}) %copy-start.3) | copy-done | bytes 196632
  37.3 4.2 %physics.1 = (f32[96,2048]{1,0:T(8,128)}, f32[1,2048]{1,0:T(1,128)}) custom-call(f32[1]{0:T(128)} %bitcast.top_ref, f32[96,2048]{1,0:T(8,128)} %get-tuple-element.10.dyn_ref, f32[24,2048]{1,0:T(8,128)} %get-tuple-element.11.own_ref, f32[24,2048]{1,0:T(8,128)} %copy-done.3, bf16[112,72]{1,0:T(8,128)(2,1)} %pad_maximum_fusion.rate_ref, ...), custom_call_target="tpu_custom_call" | custom-call | tf_op jit(solution)/shard_map/physics/pallas_call | solution.py:202
  41.5 1.3 %broadcast_in_dim.24 = f32[16,16,128]{2,1,0:T(8,128)} broadcast(f32[16,128]{1,0:T(8,128)} %bitcast.24), dimensions={1,2} | broadcast | bytes 139264 | tf_op jit(solution)/shard_map/broadcast_in_dim | solution.py:231
  42.8 6.9 %all-to-all-start = ((f32[16,16,128]{2,1,0:T(8,128)}), f32[16,16,128]{2,1,0:T(8,128)S(1)}, u32[]{:S(2)}, u32[]{:S(2)}) async-start(f32[16,16,128]{2,1,0:T(8,128)} %broadcast_in_dim.24), calls=%async_computation | async-start | bytes 262144 | tf_op jit(solution)/shard_map/all_to_all | solution.py:230
  49.7 0.6 dynamic_slice.3
  50.3 2.5 %copy.24 = f32[4,24,2048]{2,0,1:T(4,128)} copy(f32[4,24,2048]{2,1,0:T(8,128)} %bitcast.19) | data formatting | bytes 1572864 | tf_op jit(solution)/shard_map/reshape | solution.py:228
  52.8 4.7 %all-to-all-done = f32[16,16,128]{2,1,0:T(8,128)S(1)} async-done(((f32[16,16,128]{2,1,0:T(8,128)}), f32[16,16,128]{2,1,0:T(8,128)S(1)}, u32[]{:S(2)}, u32[]{:S(2)}) %all-to-all-start) | async-done | bytes 131104 | tf_op jit(solution)/shard_map/all_to_all | solution.py:230
  57.5 0.6 %copy-done = f32[16,16,128]{2,1,0:T(8,128)} copy-done((f32[16,16,128]{2,1,0:T(8,128)}, f32[16,16,128]{2,1,0:T(8,128)S(1)}, u32[]{:S(2)}) %copy-start) | copy-done | bytes 131096
  58.1 2.0 %lookup.1 = f32[1,1024]{1,0:T(1,128)} custom-call(f32[256,128]{1,0:T(8,128)} %bitcast.21, s32[1,1024]{1,0:T(1,128)} %bitcast.22), custom_call_target="tpu_custom_call" | custom-call | tf_op jit(solution)/shard_map/lookup/pallas_call | solution.py:239
  (27 shorter events, 1.9 us)
Async XLA Ops:
  0.6 0.7 %copy-start.9 = (f32[128]{0:T(128)S(1)}, f32[128]{0:T(128)}, u32[]{:S(2)}) copy-start(f32[128]{0:T(128)} %param.13) | copy-start | bytes 1540
  1.3 21.4 %collective-permute-start.2 = (f32[1,128]{1,0:T(1,128)S(1)}, f32[1,128]{1,0:T(1,128)S(1)}, u32[]{:S(2)}, u32[]{:S(2)}) collective-permute-start(f32[1,128]{1,0:T(1,128)S(1)} %bitcast.28), channel_id=1, source_target_pairs={{0,2},{2,4},{4,6},{6,8},{8,10},{10,12},{12,14},{14,16},{16,18},{18... | collective-permute-start | bytes 1544 | tf_op jit(solution)/shard_map/ppermute | solution.py:174
  4.3 18.4 %collective-permute-start.3 = (f32[1,128]{1,0:T(1,128)S(1)}, f32[1,128]{1,0:T(1,128)S(1)}, u32[]{:S(2)}, u32[]{:S(2)}) collective-permute-start(f32[1,128]{1,0:T(1,128)S(1)} %bitcast.29), channel_id=1, source_target_pairs={{2,0},{4,2},{6,4},{8,6},{10,8},{12,10},{14,12},{16,14},{18,16},{20... | collective-permute-start | bytes 1544 | tf_op jit(solution)/shard_map/ppermute | solution.py:174
  10.7 8.3 %copy-start.4 = (f32[112,20]{0,1:T(8,128)S(1)}, f32[112,20]{0,1:T(8,128)}, u32[]{:S(2)}) copy-start(f32[112,20]{0,1:T(8,128)} %param.18) | copy-start | bytes 26884
  13.4 17.1 %collective-permute-start = (f32[192,512]{1,0:T(8,128)}, f32[192,512]{1,0:T(8,128)S(1)}, u32[]{:S(2)}, u32[]{:S(2)}) collective-permute-start(f32[192,512]{1,0:T(8,128)} %get-tuple-element.9.own_ref), channel_id=1, source_target_pairs={{0,2},{2,4},{4,6},{6,8},{8,10},{10,12},{12,14},{14,16},{16,18},{18... | collective-permute-start | bytes 1179656 | tf_op jit(solution)/shard_map/ppermute | solution.py:184
  13.4 17.3 %collective-permute-start.1 = (f32[192,512]{1,0:T(8,128)}, f32[192,512]{1,0:T(8,128)S(1)}, u32[]{:S(2)}, u32[]{:S(2)}) collective-permute-start(f32[192,512]{1,0:T(8,128)} %get-tuple-element.9.own_ref), channel_id=1, source_target_pairs={{2,0},{4,2},{6,4},{8,6},{10,8},{12,10},{14,12},{16,14},{18,16},{20... | collective-permute-start | bytes 1179656 | tf_op jit(solution)/shard_map/ppermute | solution.py:185
  19.1 0.7 %copy-start.7 = (s32[4,128]{1,0:T(4,128)S(1)}, s32[4,128]{1,0:T(4,128)}, u32[]{:S(2)}) copy-start(s32[4,128]{1,0:T(4,128)} %param.14) | copy-start | bytes 6148
  19.2 0.7 %copy-start.6 = (s32[4,128]{1,0:T(4,128)S(1)}, s32[4,128]{1,0:T(4,128)}, u32[]{:S(2)}) copy-start(s32[4,128]{1,0:T(4,128)} %param.15) | copy-start | bytes 6148
  19.9 0.7 %copy-start.10 = (f32[112]{0:T(128)S(1)}, f32[112]{0:T(128)}, u32[]{:S(2)}) copy-start(f32[112]{0:T(128)} %param.17) | copy-start | bytes 1348
  21.2 0.7 %copy-start.8 = (f32[112]{0:T(128)S(1)}, f32[112]{0:T(128)}, u32[]{:S(2)}) copy-start(f32[112]{0:T(128)} %param.19) | copy-start | bytes 1348
  30.5 0.7 %copy-start.1 = (f32[192,512]{1,0:T(8,128)}, f32[192,512]{1,0:T(8,128)S(1)}, u32[]{:S(2)}) copy-start(f32[192,512]{1,0:T(8,128)S(1)} %collective-permute-done.left_ref) | copy-start | bytes 1179652
  30.7 0.8 %copy-start.2 = (f32[192,512]{1,0:T(8,128)}, f32[192,512]{1,0:T(8,128)S(1)}, u32[]{:S(2)}) copy-start(f32[192,512]{1,0:T(8,128)S(1)} %collective-permute-done.1.right_ref) | copy-start | bytes 1179652
  34.9 1.7 %collective-permute-start.4 = (f32[24,2048]{1,0:T(8,128)}, f32[24,2048]{1,0:T(8,128)S(1)}, u32[]{:S(2)}, u32[]{:S(2)}) collective-permute-start(f32[24,2048]{1,0:T(8,128)} %get-tuple-element.11.own_ref), channel_id=1, source_target_pairs={{0,1},{1,0},{2,3},{3,2},{4,5},{5,4},{6,7},{7,6},{8,9},{9,8},{10,11... | collective-permute-start | bytes 589832 | tf_op jit(solution)/shard_map/ppermute | solution.py:191
  36.6 0.7 %copy-start.3 = (f32[24,2048]{1,0:T(8,128)}, f32[24,2048]{1,0:T(8,128)S(1)}, u32[]{:S(2)}) copy-start(f32[24,2048]{1,0:T(8,128)S(1)} %collective-permute-done.4.other_ref) | copy-start | bytes 589828
  42.8 6.9 %copy-start.5 = (s32[2048]{0:T(1024)S(1)}, s32[2048]{0:T(1024)}, u32[]{:S(2)}) copy-start(s32[2048]{0:T(1024)} %param.20) | copy-start | bytes 24580
  42.8 14.7 %all-to-all-start = ((f32[16,16,128]{2,1,0:T(8,128)}), f32[16,16,128]{2,1,0:T(8,128)S(1)}, u32[]{:S(2)}, u32[]{:S(2)}) async-start(f32[16,16,128]{2,1,0:T(8,128)} %broadcast_in_dim.24), calls=%async_computation | async-start | bytes 262144 | tf_op jit(solution)/shard_map/all_to_all | solution.py:230
  57.5 0.6 %copy-start = (f32[16,16,128]{2,1,0:T(8,128)}, f32[16,16,128]{2,1,0:T(8,128)S(1)}, u32[]{:S(2)}) copy-start(f32[16,16,128]{2,1,0:T(8,128)S(1)} %all-to-all-done) | copy-start | bytes 393220

commit v2 on v1

v2 whole, which is shorter than its diff:
```python
import functools

import jax
import jax.numpy as jnp
import numpy as np
from jax import lax
from jax.experimental import pallas as pl
from jax.experimental.pallas import tpu as pltpu
from jax.sharding import PartitionSpec as P

NODES = 16
GLL_POINTS = np.array([-1.0, -1.0 / np.sqrt(5.0), 1.0 / np.sqrt(5.0), 1.0])
EDGE_NODES = ((4, 8), (13, 14), (11, 7), (2, 1))
STEP_DYN = 0.2
DEPTH_UNIT = 0.05
HEAT_SCALE = 0.1
FLUX_SCALE = 0.02
F32 = jnp.float32
BF16 = jnp.bfloat16


def derivative_matrix():
    spacing = GLL_POINTS[:, None] - GLL_POINTS[None, :]
    unit_diag = np.eye(4)
    safe_space = np.where(unit_diag > 0, 1.0, spacing)
    weights_row = np.prod(safe_space, axis=1)
    derivative = weights_row[:, None] / weights_row[None, :] / safe_space
    inverse_gap = np.where(unit_diag > 0, 0.0, 1.0 / safe_space)
    return np.where(unit_diag > 0, inverse_gap.sum(axis=1)[:, None], derivative)


def split2(x):
    high = x.astype(BF16)
    return high, (x - high.astype(F32)).astype(BF16)


def dot(a, b):
    return jnp.dot(a, b, preferred_element_type=F32)


MESH = pl.DeviceIdType.MESH
EDGES = tuple(n for pair in EDGE_NODES for n in pair)
INNER = tuple(n for n in range(NODES) if n not in EDGES)


def column(row):
    n = row.shape[1]
    same = lax.broadcasted_iota(jnp.int32, (n, n), 0) == lax.broadcasted_iota(
        jnp.int32, (n, n), 1
    )
    return jnp.sum(jnp.where(same, jnp.broadcast_to(row, (n, n)), 0.0), axis=1, keepdims=True)


def spread_rates(bands, fields):
    tracers = bands.shape[1]
    high, low = split2(-DEPTH_UNIT * bands)
    shape = (tracers, 3 * fields)
    first = lax.broadcasted_iota(jnp.int32, shape, 0) + (fields - tracers)
    lane = lax.broadcasted_iota(jnp.int32, shape, 1)
    pick_high = (lane == first) | (lane == first + fields)
    pick_low = lane == first + 2 * fields
    one = lambda m: jnp.where(m, 1.0, 0.0).astype(BF16)
    return (dot(high, one(pick_high)) + dot(low, one(pick_low))).astype(BF16)


def step_kernel(
    count,
    levels,
    x_ref,
    metric_ref,
    jac_ref,
    nbr_ref,
    side_ref,
    sun_ref,
    base_ref,
    band_ref,
    weight_ref,
    src_ref,
    out_ref,
    flux_ref,
    adv,
    edges,
    left_buf,
    right_buf,
    sq,
    other_sq,
    flux,
    table,
    edge_send,
    edge_recv,
    swap_send,
    swap_recv,
    flux_send,
    flux_recv,
):
    rows, cols = x_ref.shape
    ne = cols // NODES
    fields = rows // levels
    width = 4 * ne
    me, lev = lax.axis_index("sfc"), lax.axis_index("lev")
    after, before = lax.rem(me + 1, count), lax.rem(me + count - 1, count)

    barrier = pltpu.get_barrier_semaphore()

    def greet(step, carry):
        pl.semaphore_signal(
            barrier, inc=1, device_id=(lax.rem(me + step, count), lev), device_id_type=MESH
        )
        return carry

    lax.fori_loop(1, count, greet, 0)
    pl.semaphore_signal(barrier, inc=1, device_id=(me, 1 - lev), device_id_type=MESH)

    d = derivative_matrix()
    m0 = jnp.broadcast_to(STEP_DYN * metric_ref[0:1, :], (8, ne))
    m1 = jnp.broadcast_to(STEP_DYN * metric_ref[1:2, :], (8, ne))
    for k in range(4):
        edges[2 * rows :, k * ne : (k + 1) * ne] = jnp.broadcast_to(jac_ref[...], (8, ne))

    def advance(r, carry):
        sl = pl.ds(pl.multiple_of(r * 8, 8), 8)
        x = [x_ref[sl, n * ne : (n + 1) * ne] for n in range(NODES)]
        out = []
        for i in range(4):
            for j in range(4):
                first = sum(float(d[i, a]) * x[4 * a + j] for a in range(4))
                second = sum(float(d[j, a]) * x[4 * i + a] for a in range(4))
                out.append(x[4 * i + j] + (m0 * first + m1 * second))
        for n in INNER:
            adv[sl, n * ne : (n + 1) * ne] = out[n]
        low = pl.ds(pl.multiple_of(rows + r * 8, 8), 8)
        for k, (a, b) in enumerate(EDGE_NODES):
            edges[sl, k * ne : (k + 1) * ne] = out[b]
            edges[low, k * ne : (k + 1) * ne] = out[a]
        return carry

    lax.fori_loop(0, rows // 8, advance, 0)
    pl.semaphore_wait(barrier, count)

    to_after = pltpu.make_async_remote_copy(
        edges, left_buf, edge_send.at[0], edge_recv.at[0], device_id=(after, lev), device_id_type=MESH
    )
    to_before = pltpu.make_async_remote_copy(
        edges, right_buf, edge_send.at[1], edge_recv.at[1], device_id=(before, lev), device_id_type=MESH
    )
    to_after.start()
    to_before.start()

    def swap(half):
        return pltpu.make_async_remote_copy(
            sq.at[half],
            other_sq.at[half],
            swap_send.at[half],
            swap_recv.at[half],
            device_id=(me, 1 - lev),
            device_id_type=MESH,
        )

    def put_squares(half, slot, piece):
        squares = piece * piece
        sq[half, :, slot * ne : (slot + 1) * ne] = sum(
            squares[l * fields : (l + 1) * fields] for l in range(levels)
        )

    for slot, n in enumerate(INNER):
        put_squares(0, slot, adv[:, n * ne : (n + 1) * ne])
    inner_swap = swap(0)
    inner_swap.start()

    top = jnp.where(lev == 0, 1.0, 0.0).astype(F32)
    rates = spread_rates(band_ref[...], fields)
    base = -DEPTH_UNIT * column(base_ref[...])
    weight = column(weight_ref[...])
    whole_light = jnp.sum(weight)

    total_nodes = count * ne
    near = nbr_ref[...] - (me - 1) * ne
    near = jnp.where(near < 0, near + total_nodes, near)
    near = jnp.where(near >= total_nodes, near - total_nodes, near)
    window = jnp.where(near >= ne, 1, 0) + jnp.where(near >= 2 * ne, 1, 0)
    spot = window * (width - ne) + side_ref[...] * ne + near
    target = jnp.concatenate([spot[k : k + 1, :] for k in range(4)], axis=1)

    def gather(ref, w):
        lanes = lax.broadcasted_iota(jnp.int32, (width, width), 0) + w * width
        onehot = jnp.where(lanes == target, 1.0, 0.0).astype(BF16)
        high, low = split2(ref[...])
        return dot(high, onehot) + dot(low, onehot)

    def light(sums, times):
        high = sums.astype(BF16).astype(F32)
        stacked = jnp.concatenate([high, sums - high, high], axis=0).astype(BF16)
        depth = dot(rates, stacked) + times * base
        return jnp.sum(weight * jnp.exp(depth), axis=0, keepdims=True)

    def radiate(half, slots, nodes, pieces):
        lanes = slice(slots[0] * ne, (slots[-1] + 1) * ne)
        join = lambda parts: jnp.concatenate(parts, axis=1)
        sun = jnp.maximum(join([sun_ref[:, n * ne : (n + 1) * ne] for n in nodes]), 0.0)
        other = other_sq[half, :, lanes]
        extra = light(other + top * sq[half, :, lanes], levels * (1.0 + top))
        above = top * whole_light + (1.0 - top) * extra
        running = (1.0 - top) * other
        for l in range(levels):
            part = join([p[l * fields : (l + 1) * fields, :] for p in pieces])
            running = running + part * part
            below = light(running, (1.0 - top) * levels + (l + 1.0))
            heat = HEAT_SCALE * sun * (above - below)
            row = l * fields + 2
            for s, n in enumerate(nodes):
                out_ref[row : row + 1, n * ne : (n + 1) * ne] = (
                    pieces[s][row : row + 1, :] + heat[:, s * ne : (s + 1) * ne]
                )
            above = below
        ground = FLUX_SCALE * sun * (top * extra + (1.0 - top) * above)
        for s, n in enumerate(nodes):
            flux[n : n + 1, :] = ground[:, s * ne : (s + 1) * ne]

    acc = gather(edges, 1)
    inner_swap.wait()
    for part in range(2):
        slots = range(part * 4, part * 4 + 4)
        nodes = [INNER[s] for s in slots]
        pieces = [adv[:, n * ne : (n + 1) * ne] for n in nodes]
        for n, piece in zip(nodes, pieces):
            out_ref[:, n * ne : (n + 1) * ne] = piece
        radiate(0, slots, nodes, pieces)

    to_after.wait()
    acc = acc + gather(left_buf, 0)
    to_before.wait()
    acc = acc + gather(right_buf, 2)

    own_jac = jnp.concatenate([jac_ref[...]] * 4, axis=1)
    far_jac = acc[2 * rows : 2 * rows + 1, :]
    total = own_jac + far_jac
    own_part, far_part = own_jac / total, far_jac / total
    first = own_part * edges[rows : 2 * rows, :] + far_part * acc[:rows]
    second = own_part * edges[:rows, :] + far_part * acc[rows : 2 * rows]
    sets = ((first, [a for a, _ in EDGE_NODES]), (second, [b for _, b in EDGE_NODES]))
    for part, (values, nodes) in enumerate(sets):
        for k, n in enumerate(nodes):
            piece = values[:, k * ne : (k + 1) * ne]
            put_squares(1, part * 4 + k, piece)
            out_ref[:, n * ne : (n + 1) * ne] = piece
    edge_swap = swap(1)
    edge_swap.start()
    edge_swap.wait()
    for part, (_, nodes) in enumerate(sets):
        slots = range(part * 4, part * 4 + 4)
        radiate(1, slots, nodes, [out_ref[:, n * ne : (n + 1) * ne] for n in nodes])

    def send(step):
        return pltpu.make_async_remote_copy(
            flux,
            table.at[me],
            flux_send.at[step],
            flux_recv.at[me],
            device_id=(lax.rem(me + step, count), lev),
            device_id_type=MESH,
        )

    def arrive(step):
        peer = lax.rem(me + step, count)
        return pltpu.make_async_remote_copy(
            flux,
            table.at[peer],
            flux_send.at[step],
            flux_recv.at[peer],
            device_id=(peer, lev),
            device_id_type=MESH,
        )

    def start_send(step, carry):
        send(step).start()
        return carry

    def finish(step, carry):
        send(step).wait_send()
        arrive(step).wait_recv()
        return carry

    lax.fori_loop(1, count, start_send, 0)
    table[me] = flux[...]
    taken = flux_ref.shape[1]
    index = src_ref[:, pl.ds(pl.multiple_of(lev * taken, 128), taken)]
    high_index, lane_index = index >> 7, index & 127
    lines = count * cols // 128
    onehot = jnp.where(
        lax.broadcasted_iota(jnp.int32, (lines, taken), 0) == high_index, 1.0, 0.0
    ).astype(BF16)
    mask = lax.broadcasted_iota(jnp.int32, (128, taken), 0) == lane_index
    lax.fori_loop(1, count, finish, 0)
    values = table[...].reshape(lines, 128).T
    high, _ = split2(values)
    low, tail = split2(values - high.astype(F32))
    picked = dot(high, onehot) + dot(low, onehot) + dot(tail, onehot)
    flux_ref[...] = jnp.sum(jnp.where(mask, picked, 0.0), axis=0, keepdims=True)


def local(
    air_state,
    metric,
    jacobian,
    edge_nbr,
    edge_side,
    coszen,
    kappa_base,
    band_kappa,
    solar_weight,
    stretch_pos,
    stretch_src,
):
    fields, levels, cols = air_state.shape
    ne = cols // NODES
    rows = fields * levels
    count = lax.axis_size("sfc")
    part = cols // lax.axis_size("lev")
    state = air_state.transpose(1, 0, 2).reshape(rows, cols)
    vmem = pl.BlockSpec(memory_space=pltpu.VMEM)
    new, flux = pl.pallas_call(
        functools.partial(step_kernel, count, levels),
        in_specs=[vmem] * 10,
        out_specs=(vmem, vmem),
        out_shape=(
            jax.ShapeDtypeStruct((rows, cols), F32),
            jax.ShapeDtypeStruct((1, part), F32),
        ),
        scratch_shapes=[
            pltpu.VMEM((rows, cols), F32),
            pltpu.VMEM((2 * rows + 8, 4 * ne), F32),
            pltpu.VMEM((2 * rows + 8, 4 * ne), F32),
            pltpu.VMEM((2 * rows + 8, 4 * ne), F32),
            pltpu.VMEM((2, fields, cols // 2), F32),
            pltpu.VMEM((2, fields, cols // 2), F32),
            pltpu.VMEM((NODES, ne), F32),
            pltpu.VMEM((count, NODES, ne), F32),
            pltpu.SemaphoreType.DMA((2,)),
            pltpu.SemaphoreType.DMA((2,)),
            pltpu.SemaphoreType.DMA((2,)),
            pltpu.SemaphoreType.DMA((2,)),
            pltpu.SemaphoreType.DMA((count,)),
            pltpu.SemaphoreType.DMA((count,)),
        ],
        compiler_params=pltpu.CompilerParams(collective_id=0, has_side_effects=True),
        name="step",
    )(
        state,
        metric,
        jacobian[None, :],
        edge_nbr,
        edge_side,
        coszen[None, :],
        kappa_base[None, :],
        band_kappa,
        solar_weight[None, :],
        stretch_src[None, :],
    )
    new_state = new.reshape(levels, fields, cols).transpose(1, 0, 2)
    return (new_state, flux.reshape(part))


def solution(mesh):
    return jax.shard_map(
        local,
        mesh=mesh,
        in_specs=(
            P(None, "lev", "sfc"),
            P(None, "sfc"),
            P("sfc"),
            P(None, "sfc"),
            P(None, "sfc"),
            P("sfc"),
            P(),
            P(),
            P(),
            P("sfc"),
            P("sfc"),
        ),
        out_specs=(P(None, "lev", "sfc"), P(("sfc", "lev"))),
        check_vma=False,
    )
```

time: 60.7 us -> 42.9 us (0.71)
  Pallas kernels: 12.3 us -> 34.9 us
  starting transfers between devices: 19.4 us -> 0 us
  waiting for transfers between devices: 13.1 us -> 0 us
  local copies, waits for them, and re-layouts: 12.6 us -> 7.01 us
  other arithmetic: 1.98 us -> 0 us
    pallas_call x4 -> x1, Pallas kernels: 12.3 us -> 34.9 us  [local(): pl.pallas_call(functools.partial(step_kernel, count, levels), in_specs=[v...]
    ppermute x5 -> x0, starting transfers between devices: 12.6 us -> none  [the longest x1 5.62 us: local(): right = lax.ppermute(edges, 'sfc', backward)]
    ppermute x5 -> x0, waiting for transfers between devices: 8.38 us -> none  [the longest x1 7.31 us: local(): left = lax.ppermute(edges, 'sfc', forward)]
    all_to_all x1 -> x0, starting transfers between devices: 6.85 us -> none  [local(): lax.all_to_all(jnp.broadcast_to(flux.reshape(1, cols // 128, 128), (count...]
    all_to_all x1 -> x0, waiting for transfers between devices: 4.67 us -> none  [local(): lax.all_to_all(jnp.broadcast_to(flux.reshape(1, cols // 128, 128), (count...]
    unnamed x23 -> x4, local copies, waits for them, and re-layouts: 4.22 us -> 2.02 us
    broadcast_in_dim x2 -> x0, local copies, waits for them, and re-layouts: 2.08 us -> none  [the longest x1 1.35 us: local(): jnp.broadcast_to(flux.reshape(1, cols // 128, 128), (count, cols // 128,...]
    concatenate x2 -> x0, other arithmetic: 1.28 us -> none  [the longest x1 0.69 us: local(): stacked_rates = jnp.concatenate([high, high, low], axis=1).astype(BF16)]
  transfers between devices with their start and end apart: 6 -> 0, of which waited for: 4 -> 0; matrix products, arithmetic and copies ran while one was open for 15% -> 0% of each run, Pallas kernels for 4% -> 0%
where the time goes in v2:
time: 42.9 us; the launch traced here: 42.6 us
  Pallas kernels  34.9 us (81%)
  local copies, waits for them, and re-layouts  7.01 us (16%)
  between operations  0.65 us (2%)
    pallas_call x1, Pallas kernels, local(): pl.pallas_call(functools.partial(step_kernel, count, levels), in_specs=[v...  34.9 us
    reshape x1, local copies, waits for them, and re-layouts, local(): new_state = new.reshape(levels, fields, cols).transpose(1, 0, 2)  2.52 us
    transpose x1, local copies, waits for them, and re-layouts, local(): state = air_state.transpose(1, 0, 2).reshape(rows, cols)  2.47 us
    unnamed x4, local copies, waits for them, and re-layouts  2.02 us

profile of v2, /device:TPU:0, one launch (start us, length us, event | category | flops | bytes accessed | tf_op | source)
XLA Modules:
  0.0 42.6 jit_solution(15035186199282496030)
XLA Ops:
  0.6 1.4 %copy.13.band_ref = f32[112,20]{1,0:T(8,128)} copy(f32[112,20]{0,1:T(8,128)} %param.18) | data formatting | bytes 17920 | tf_op args[7]
  2.1 2.5 %copy.12 = f32[4,24,2048]{2,1,0:T(8,128)} copy(f32[4,24,2048]{2,0,1:T(4,128)} %bitcast.13) | data formatting | bytes 1572864 | tf_op jit(solution)/shard_map/transpose | solution.py:319
  4.5 34.9 %step.1 = (f32[96,2048]{1,0:T(8,128)}, f32[1,1024]{1,0:T(1,128)}) custom-call(f32[96,2048]{1,0:T(8,128)} %bitcast.12, f32[2,128]{1,0:T(2,128)} %metric_ref.1, f32[1,128]{1,0:T(1,128)} %bitcast.19, s32[4,128]{1,0:T(4,128)} %nbr_ref.1, s32[4,128]{1,0:T(4,128)} %side_ref.1, f32[1,2048]{1,0:T(1,128)} %bitcast.16, f32[1,112]{1,0:T(1,128)} %bitcast.20, ...), custom_call_target="tpu_custom_call" | custom-call | tf_op jit(solution)/shard_map/step/pallas_call | solution.py:321
  39.5 0.0 copy-start
  39.5 2.5 %copy.16 = f32[4,24,2048]{2,0,1:T(4,128)} copy(f32[4,24,2048]{2,1,0:T(8,128)} %bitcast.15) | data formatting | bytes 1572864 | tf_op jit(solution)/shard_map/reshape | solution.py:359
  42.0 0.0 copy-done
  42.0 0.6 %copy.18 = f32[1024]{0:T(1024)} copy(f32[1024]{0:T(1024)S(1)} %bitcast.18) | data formatting | bytes 8192
Async XLA Ops:
  39.5 2.5 %copy-start = (f32[1,1024]{1,0:T(1,128)S(1)}, f32[1,1024]{1,0:T(1,128)}, u32[]{:S(2)}) copy-start(f32[1,1024]{1,0:T(1,128)} %get-tuple-element.5) | copy-start | bytes 12292

commit v3 on v2

--- a/solution.py
+++ b/solution.py
@@ -52,7 +52,7 @@
 
 
 def spread_rates(bands, fields):
-    tracers = bands.shape[1]
+    tracers = bands.shape[0]
     high, low = split2(-DEPTH_UNIT * bands)
     shape = (tracers, 3 * fields)
     first = lax.broadcasted_iota(jnp.int32, shape, 0) + (fields - tracers)
@@ -60,7 +60,8 @@
     pick_high = (lane == first) | (lane == first + fields)
     pick_low = lane == first + 2 * fields
     one = lambda m: jnp.where(m, 1.0, 0.0).astype(BF16)
-    return (dot(high, one(pick_high)) + dot(low, one(pick_low))).astype(BF16)
+    mix = lambda a, b: lax.dot_general(a, b, (((0,), (0,)), ((), ())), preferred_element_type=F32)
+    return (mix(high, one(pick_high)) + mix(low, one(pick_low))).astype(BF16)
 
 
 def step_kernel(
@@ -80,8 +81,8 @@
     flux_ref,
     adv,
     edges,
-    left_buf,
-    right_buf,
+    direct_buf,
+    relay_buf,
     sq,
     other_sq,
     flux,
@@ -98,7 +99,9 @@
     fields = rows // levels
     width = 4 * ne
     me, lev = lax.axis_index("sfc"), lax.axis_index("lev")
-    after, before = lax.rem(me + 1, count), lax.rem(me + count - 1, count)
+    odd = lax.rem(me, 2)
+    partner = me + 1 - 2 * odd
+    onward = lax.rem(me + count + 2 - 4 * odd, count)
 
     barrier = pltpu.get_barrier_semaphore()
 
@@ -115,36 +118,56 @@
     m0 = jnp.broadcast_to(STEP_DYN * metric_ref[0:1, :], (8, ne))
     m1 = jnp.broadcast_to(STEP_DYN * metric_ref[1:2, :], (8, ne))
     for k in range(4):
-        edges[2 * rows :, k * ne : (k + 1) * ne] = jnp.broadcast_to(jac_ref[...], (8, ne))
-
-    def advance(r, carry):
-        sl = pl.ds(pl.multiple_of(r * 8, 8), 8)
-        x = [x_ref[sl, n * ne : (n + 1) * ne] for n in range(NODES)]
-        out = []
-        for i in range(4):
-            for j in range(4):
-                first = sum(float(d[i, a]) * x[4 * a + j] for a in range(4))
-                second = sum(float(d[j, a]) * x[4 * i + a] for a in range(4))
-                out.append(x[4 * i + j] + (m0 * first + m1 * second))
-        for n in INNER:
-            adv[sl, n * ne : (n + 1) * ne] = out[n]
-        low = pl.ds(pl.multiple_of(rows + r * 8, 8), 8)
-        for k, (a, b) in enumerate(EDGE_NODES):
-            edges[sl, k * ne : (k + 1) * ne] = out[b]
-            edges[low, k * ne : (k + 1) * ne] = out[a]
-        return carry
-
-    lax.fori_loop(0, rows // 8, advance, 0)
-    pl.semaphore_wait(barrier, count)
-
-    to_after = pltpu.make_async_remote_copy(
-        edges, left_buf, edge_send.at[0], edge_recv.at[0], device_id=(after, lev), device_id_type=MESH
-    )
-    to_before = pltpu.make_async_remote_copy(
-        edges, right_buf, edge_send.at[1], edge_recv.at[1], device_id=(before, lev), device_id_type=MESH
-    )
-    to_after.start()
-    to_before.start()
+        edges[:8, k * ne : (k + 1) * ne] = jnp.broadcast_to(jac_ref[...], (8, ne))
+
+    def chunk(l):
+        return slice(0 if l == 0 else 8 + 2 * fields * l, 8 + 2 * fields * (l + 1))
+
+    def direct(l):
+        return pltpu.make_async_remote_copy(
+            edges.at[chunk(l)],
+            direct_buf.at[chunk(l)],
+            edge_send.at[0, l],
+            edge_recv.at[0, l],
+            device_id=(partner, lev),
+            device_id_type=MESH,
+        )
+
+    def relay(l):
+        return pltpu.make_async_remote_copy(
+            direct_buf.at[chunk(l)],
+            relay_buf.at[chunk(l)],
+            edge_send.at[1, l],
+            edge_recv.at[1, l],
+            device_id=(onward, lev),
+            device_id_type=MESH,
+        )
+
+    for l in range(levels):
+
+        def advance(r, carry, l=l):
+            sl = pl.ds(pl.multiple_of(l * fields + r * 8, 8), 8)
+            x = [x_ref[sl, n * ne : (n + 1) * ne] for n in range(NODES)]
+            out = []
+            for i in range(4):
+                for j in range(4):
+                    one = sum(float(d[i, a]) * x[4 * a + j] for a in range(4))
+                    two = sum(float(d[j, a]) * x[4 * i + a] for a in range(4))
+                    out.append(x[4 * i + j] + (m0 * one + m1 * two))
+            for n in INNER:
+                adv[sl, n * ne : (n + 1) * ne] = out[n]
+            start = 8 + 2 * fields * l + r * 8
+            seconds = pl.ds(pl.multiple_of(start, 8), 8)
+            firsts = pl.ds(pl.multiple_of(start + fields, 8), 8)
+            for k, (a, b) in enumerate(EDGE_NODES):
+                edges[seconds, k * ne : (k + 1) * ne] = out[b]
+                edges[firsts, k * ne : (k + 1) * ne] = out[a]
+            return carry
+
+        lax.fori_loop(0, fields // 8, advance, 0)
+        if l == 0:
+            pl.semaphore_wait(barrier, count)
+        direct(l).start()
 
     def swap(half):
         return pltpu.make_async_remote_copy(
@@ -181,10 +204,12 @@
     spot = window * (width - ne) + side_ref[...] * ne + near
     target = jnp.concatenate([spot[k : k + 1, :] for k in range(4)], axis=1)
 
-    def gather(ref, w):
+    def choice(w):
         lanes = lax.broadcasted_iota(jnp.int32, (width, width), 0) + w * width
-        onehot = jnp.where(lanes == target, 1.0, 0.0).astype(BF16)
-        high, low = split2(ref[...])
+        return jnp.where(lanes == target, 1.0, 0.0).astype(BF16)
+
+    def gather(ref, onehot, l):
+        high, low = split2(ref[chunk(l)])
         return dot(high, onehot) + dot(low, onehot)
 
     def light(sums, times):
@@ -216,7 +241,13 @@
         for s, n in enumerate(nodes):
             flux[n : n + 1, :] = ground[:, s * ne : (s + 1) * ne]
 
-    acc = gather(edges, 1)
+    def forward(l):
+        direct(l).wait_recv()
+        relay(l).start()
+
+    own_choice = choice(1)
+    acc = [gather(edges, own_choice, l) for l in range(levels)]
+    forward(0)
     inner_swap.wait()
     for part in range(2):
         slots = range(part * 4, part * 4 + 4)
@@ -225,28 +256,46 @@
         for n, piece in zip(nodes, pieces):
             out_ref[:, n * ne : (n + 1) * ne] = piece
         radiate(0, slots, nodes, pieces)
-
-    to_after.wait()
-    acc = acc + gather(left_buf, 0)
-    to_before.wait()
-    acc = acc + gather(right_buf, 2)
-
-    own_jac = jnp.concatenate([jac_ref[...]] * 4, axis=1)
-    far_jac = acc[2 * rows : 2 * rows + 1, :]
-    total = own_jac + far_jac
-    own_part, far_part = own_jac / total, far_jac / total
-    first = own_part * edges[rows : 2 * rows, :] + far_part * acc[:rows]
-    second = own_part * edges[:rows, :] + far_part * acc[rows : 2 * rows]
-    sets = ((first, [a for a, _ in EDGE_NODES]), (second, [b for _, b in EDGE_NODES]))
-    for part, (values, nodes) in enumerate(sets):
-        for k, n in enumerate(nodes):
-            piece = values[:, k * ne : (k + 1) * ne]
-            put_squares(1, part * 4 + k, piece)
-            out_ref[:, n * ne : (n + 1) * ne] = piece
+        if part == 0:
+            forward(1)
+
+    direct_choice, relay_choice = choice(2 - 2 * odd), choice(2 * odd)
+    for l in range(levels):
+        if l > 1:
+            forward(l)
+        acc[l] = acc[l] + gather(direct_buf, direct_choice, l)
+
+    firsts = [a for a, _ in EDGE_NODES]
+    seconds = [b for _, b in EDGE_NODES]
+    sums = [0.0, 0.0]
+    for l in range(levels):
+        relay(l).wait_recv()
+        far = acc[l] + gather(relay_buf, relay_choice, l)
+        if l == 0:
+            own_jac = jnp.concatenate([jac_ref[...]] * 4, axis=1)
+            far_jac = far[0:1, :]
+            far = far[8:]
+            total = own_jac + far_jac
+            own_part, far_part = own_jac / total, far_jac / total
+        start = 8 + 2 * fields * l
+        own_second = edges[start : start + fields, :]
+        own_first = edges[start + fields : start + 2 * fields, :]
+        both = (
+            (own_part * own_first + far_part * far[:fields], firsts),
+            (own_part * own_second + far_part * far[fields:], seconds),
+        )
+        for p, (values, nodes) in enumerate(both):
+            sums[p] = sums[p] + values * values
+            for k, n in enumerate(nodes):
+                out_ref[l * fields : (l + 1) * fields, n * ne : (n + 1) * ne] = values[
+                    :, k * ne : (k + 1) * ne
+                ]
+    sq[1, :, :width] = sums[0]
+    sq[1, :, width:] = sums[1]
     edge_swap = swap(1)
     edge_swap.start()
     edge_swap.wait()
-    for part, (_, nodes) in enumerate(sets):
+    for part, nodes in enumerate((firsts, seconds)):
         slots = range(part * 4, part * 4 + 4)
         radiate(1, slots, nodes, [out_ref[:, n * ne : (n + 1) * ne] for n in nodes])
 
@@ -291,6 +340,9 @@
     ).astype(BF16)
     mask = lax.broadcasted_iota(jnp.int32, (128, taken), 0) == lane_index
     lax.fori_loop(1, count, finish, 0)
+    for l in range(levels):
+        direct(l).wait_send()
+        relay(l).wait_send()
     values = table[...].reshape(lines, 128).T
     high, _ = split2(values)
     low, tail = split2(values - high.astype(F32))
@@ -335,8 +387,8 @@
             pltpu.VMEM((2, fields, cols // 2), F32),
             pltpu.VMEM((NODES, ne), F32),
             pltpu.VMEM((count, NODES, ne), F32),
-            pltpu.SemaphoreType.DMA((2,)),
-            pltpu.SemaphoreType.DMA((2,)),
+            pltpu.SemaphoreType.DMA((2, levels)),
+            pltpu.SemaphoreType.DMA((2, levels)),
             pltpu.SemaphoreType.DMA((2,)),
             pltpu.SemaphoreType.DMA((2,)),
             pltpu.SemaphoreType.DMA((count,)),
@@ -352,7 +404,7 @@
         edge_side,
         coszen[None, :],
         kappa_base[None, :],
-        band_kappa,
+        band_kappa.T,
         solar_weight[None, :],
         stretch_src[None, :],
     )

time: 42.9 us -> 38.3 us (0.89)
  Pallas kernels: 34.9 us -> 31.9 us
  local copies, waits for them, and re-layouts: 7.01 us -> 5.59 us
    pallas_call x1, Pallas kernels: 34.9 us -> 31.9 us  [local(): pl.pallas_call(functools.partial(step_kernel, count, levels), in_specs=[v...]
    unnamed x4 -> x3, local copies, waits for them, and re-layouts: 2.02 us -> 0.6 us
where the time goes in v3:
time: 38.3 us; the launch traced here: 38.1 us
  Pallas kernels  31.9 us (83%)
  local copies, waits for them, and re-layouts  5.59 us (15%)
  between operations  0.65 us (2%)
    pallas_call x1, Pallas kernels, local(): pl.pallas_call(functools.partial(step_kernel, count, levels), in_specs=[v...  31.9 us
    reshape x1, local copies, waits for them, and re-layouts, local(): new_state = new.reshape(levels, fields, cols).transpose(1, 0, 2)  2.52 us
    transpose x1, local copies, waits for them, and re-layouts, local(): state = air_state.transpose(1, 0, 2).reshape(rows, cols)  2.47 us

profile of v3, /device:TPU:0, one launch (start us, length us, event | category | flops | bytes accessed | tf_op | source)
XLA Modules:
  0.0 38.1 jit_solution(13810337339262042645)
XLA Ops:
  0.6 2.5 %copy.12 = f32[4,24,2048]{2,1,0:T(8,128)} copy(f32[4,24,2048]{2,0,1:T(4,128)} %bitcast.14) | data formatting | bytes 1572864 | tf_op jit(solution)/shard_map/transpose | solution.py:371
  3.1 31.9 %step.1 = (f32[96,2048]{1,0:T(8,128)}, f32[1,1024]{1,0:T(1,128)}) custom-call(f32[96,2048]{1,0:T(8,128)} %bitcast.13, f32[2,128]{1,0:T(2,128)} %metric_ref.1, f32[1,128]{1,0:T(1,128)} %bitcast.21, s32[4,128]{1,0:T(4,128)} %nbr_ref.1, s32[4,128]{1,0:T(4,128)} %side_ref.1, f32[1,2048]{1,0:T(1,128)} %bitcast.18, f32[1,112]{1,0:T(1,128)} %bitcast.22, ...), custom_call_target="tpu_custom_call" | custom-call | tf_op jit(solution)/shard_map/step/pallas_call | solution.py:373
  35.0 0.0 copy-start
  35.0 2.5 %copy.15 = f32[4,24,2048]{2,0,1:T(4,128)} copy(f32[4,24,2048]{2,1,0:T(8,128)} %bitcast.16) | data formatting | bytes 1572864 | tf_op jit(solution)/shard_map/reshape | solution.py:411
  37.5 0.0 copy-done
  37.5 0.6 %copy.17 = f32[1024]{0:T(1024)} copy(f32[1024]{0:T(1024)S(1)} %bitcast.20) | data formatting | bytes 8192
Async XLA Ops:
  35.0 2.5 %copy-start = (f32[1,1024]{1,0:T(1,128)S(1)}, f32[1,1024]{1,0:T(1,128)}, u32[]{:S(2)}) copy-start(f32[1,1024]{1,0:T(1,128)} %get-tuple-element.5) | copy-start | bytes 12292

commit v4 on v3

--- a/solution.py
+++ b/solution.py
@@ -67,7 +67,7 @@
 def step_kernel(
     count,
     levels,
-    x_ref,
+    state_ref,
     metric_ref,
     jac_ref,
     nbr_ref,
@@ -77,8 +77,10 @@
     band_ref,
     weight_ref,
     src_ref,
+    new_ref,
+    flux_ref,
+    x_ref,
     out_ref,
-    flux_ref,
     adv,
     edges,
     direct_buf,
@@ -93,6 +95,8 @@
     swap_recv,
     flux_send,
     flux_recv,
+    in_sem,
+    out_sem,
 ):
     rows, cols = x_ref.shape
     ne = cols // NODES
@@ -103,6 +107,18 @@
     partner = me + 1 - 2 * odd
     onward = lax.rem(me + count + 2 - 4 * odd, count)
 
+    def fetch(l):
+        return pltpu.make_async_copy(
+            state_ref.at[:, l, :], x_ref.at[l * fields : (l + 1) * fields], in_sem.at[l]
+        )
+
+    def store(l):
+        return pltpu.make_async_copy(
+            out_ref.at[l * fields : (l + 1) * fields], new_ref.at[:, l, :], out_sem.at[l]
+        )
+
+    for l in range(levels):
+        fetch(l).start()
     barrier = pltpu.get_barrier_semaphore()
 
     def greet(step, carry):
@@ -164,6 +180,7 @@
                 edges[firsts, k * ne : (k + 1) * ne] = out[a]
             return carry
 
+        fetch(l).wait()
         lax.fori_loop(0, fields // 8, advance, 0)
         if l == 0:
             pl.semaphore_wait(barrier, count)
@@ -330,6 +347,8 @@
         return carry
 
     lax.fori_loop(1, count, start_send, 0)
+    for l in range(levels):
+        store(l).start()
     table[me] = flux[...]
     taken = flux_ref.shape[1]
     index = src_ref[:, pl.ds(pl.multiple_of(lev * taken, 128), taken)]
@@ -341,6 +360,7 @@
     mask = lax.broadcasted_iota(jnp.int32, (128, taken), 0) == lane_index
     lax.fori_loop(1, count, finish, 0)
     for l in range(levels):
+        store(l).wait()
         direct(l).wait_send()
         relay(l).wait_send()
     values = table[...].reshape(lines, 128).T
@@ -368,17 +388,19 @@
     rows = fields * levels
     count = lax.axis_size("sfc")
     part = cols // lax.axis_size("lev")
-    state = air_state.transpose(1, 0, 2).reshape(rows, cols)
+    anywhere = pl.BlockSpec(memory_space=pl.ANY)
     vmem = pl.BlockSpec(memory_space=pltpu.VMEM)
     new, flux = pl.pallas_call(
         functools.partial(step_kernel, count, levels),
-        in_specs=[vmem] * 10,
-        out_specs=(vmem, vmem),
+        in_specs=[anywhere] + [vmem] * 9,
+        out_specs=(anywhere, vmem),
         out_shape=(
-            jax.ShapeDtypeStruct((rows, cols), F32),
+            jax.ShapeDtypeStruct(air_state.shape, F32),
             jax.ShapeDtypeStruct((1, part), F32),
         ),
         scratch_shapes=[
+            pltpu.VMEM((rows, cols), F32),
+            pltpu.VMEM((rows, cols), F32),
             pltpu.VMEM((rows, cols), F32),
             pltpu.VMEM((2 * rows + 8, 4 * ne), F32),
             pltpu.VMEM((2 * rows + 8, 4 * ne), F32),
@@ -393,11 +415,13 @@
             pltpu.SemaphoreType.DMA((2,)),
             pltpu.SemaphoreType.DMA((count,)),
             pltpu.SemaphoreType.DMA((count,)),
+            pltpu.SemaphoreType.DMA((levels,)),
+            pltpu.SemaphoreType.DMA((levels,)),
         ],
         compiler_params=pltpu.CompilerParams(collective_id=0, has_side_effects=True),
         name="step",
     )(
-        state,
+        air_state,
         metric,
         jacobian[None, :],
         edge_nbr,
@@ -408,8 +432,7 @@
         solar_weight[None, :],
         stretch_src[None, :],
     )
-    new_state = new.reshape(levels, fields, cols).transpose(1, 0, 2)
-    return (new_state, flux.reshape(part))
+    return (new, flux.reshape(part))
 
 
 def solution(mesh):

time: 38.3 us -> 35.1 us (0.916)
  local copies, waits for them, and re-layouts: 5.59 us -> 2.69 us
    reshape x1 -> x0, local copies, waits for them, and re-layouts: 2.52 us -> none  [local(): new_state = new.reshape(levels, fields, cols).transpose(1, 0, 2)]
    transpose x1 -> x0, local copies, waits for them, and re-layouts: 2.47 us -> none  [local(): state = air_state.transpose(1, 0, 2).reshape(rows, cols)]
    unnamed x3 -> x4, local copies, waits for them, and re-layouts: 0.6 us -> 2.69 us
where the time goes in v4:
time: 35.1 us; the launch traced here: 34.9 us
  Pallas kernels  31.6 us (90%)
  local copies, waits for them, and re-layouts  2.69 us (8%)
  between operations  0.65 us (2%)
    pallas_call x1, Pallas kernels, local(): pl.pallas_call(functools.partial(step_kernel, count, levels), in_specs=[a...  31.6 us
    unnamed x4, local copies, waits for them, and re-layouts  2.69 us

profile of v4, /device:TPU:0, one launch (start us, length us, event | category | flops | bytes accessed | tf_op | source)
XLA Modules:
  0.0 34.9 jit_solution(8674221173052303745)
XLA Ops:
  0.6 31.6 %step.1 = (f32[24,4,2048]{2,1,0:T(4,128)}, f32[1,1024]{1,0:T(1,128)}) custom-call(f32[24,4,2048]{2,1,0:T(4,128)} %state_ref.1, f32[2,128]{1,0:T(2,128)} %metric_ref.1, f32[1,128]{1,0:T(1,128)} %bitcast.11, s32[4,128]{1,0:T(4,128)} %nbr_ref.1, s32[4,128]{1,0:T(4,128)} %side_ref.1, f32[1,2048]{1,0:T(1,128)} %bitcast.8, f32[1,112]{1,0:T(1,128)} %bitcast.12, ...), custom_call_target="tpu_custom_call" | custom-call | tf_op jit(solution)/shard_map/step/pallas_call | solution.py:393
  32.2 0.0 copy-start
  32.2 2.1 %copy.14 = f32[24,4,2048]{2,1,0:T(4,128)} copy(f32[24,4,2048]{2,1,0:T(4,128)} %get-tuple-element.8) | data formatting | bytes 1572864
  34.3 0.0 copy-done
  34.3 0.6 %copy.15 = f32[1024]{0:T(1024)} copy(f32[1024]{0:T(1024)S(1)} %bitcast.10) | data formatting | bytes 8192
Async XLA Ops:
  32.2 2.1 %copy-start = (f32[1,1024]{1,0:T(1,128)S(1)}, f32[1,1024]{1,0:T(1,128)}, u32[]{:S(2)}) copy-start(f32[1,1024]{1,0:T(1,128)} %get-tuple-element.5) | copy-start | bytes 12292

commit v5 on v4

--- a/solution.py
+++ b/solution.py
@@ -229,24 +229,33 @@
         high, low = split2(ref[chunk(l)])
         return dot(high, onehot) + dot(low, onehot)
 
-    def light(sums, times):
+    def depth_of(sums):
         high = sums.astype(BF16).astype(F32)
         stacked = jnp.concatenate([high, sums - high, high], axis=0).astype(BF16)
-        depth = dot(rates, stacked) + times * base
-        return jnp.sum(weight * jnp.exp(depth), axis=0, keepdims=True)
-
-    def radiate(half, slots, nodes, pieces):
-        lanes = slice(slots[0] * ne, (slots[-1] + 1) * ne)
-        join = lambda parts: jnp.concatenate(parts, axis=1)
-        sun = jnp.maximum(join([sun_ref[:, n * ne : (n + 1) * ne] for n in nodes]), 0.0)
-        other = other_sq[half, :, lanes]
-        extra = light(other + top * sq[half, :, lanes], levels * (1.0 + top))
-        above = top * whole_light + (1.0 - top) * extra
-        running = (1.0 - top) * other
+        return dot(rates, stacked)
+
+    def light(depth, times):
+        return jnp.sum(weight * jnp.exp(depth + times * base), axis=0, keepdims=True)
+
+    join = lambda parts: jnp.concatenate(parts, axis=1)
+
+    def own_depths(pieces):
+        running, depths = 0.0, []
         for l in range(levels):
             part = join([p[l * fields : (l + 1) * fields, :] for p in pieces])
             running = running + part * part
-            below = light(running, (1.0 - top) * levels + (l + 1.0))
+            depths.append(depth_of(running))
+        return depths
+
+    def radiate(half, slots, nodes, pieces, depths):
+        lanes = slice(slots[0] * ne, (slots[-1] + 1) * ne)
+        sun = jnp.maximum(join([sun_ref[:, n * ne : (n + 1) * ne] for n in nodes]), 0.0)
+        other = depth_of(other_sq[half, :, lanes])
+        extra = light(other + top * depths[-1], levels * (1.0 + top))
+        above = top * whole_light + (1.0 - top) * extra
+        other = (1.0 - top) * other
+        for l in range(levels):
+            below = light(other + depths[l], (1.0 - top) * levels + (l + 1.0))
             heat = HEAT_SCALE * sun * (above - below)
             row = l * fields + 2
             for s, n in enumerate(nodes):
@@ -272,7 +281,7 @@
         pieces = [adv[:, n * ne : (n + 1) * ne] for n in nodes]
         for n, piece in zip(nodes, pieces):
             out_ref[:, n * ne : (n + 1) * ne] = piece
-        radiate(0, slots, nodes, pieces)
+        radiate(0, slots, nodes, pieces, own_depths(pieces))
         if part == 0:
             forward(1)
 
@@ -311,10 +320,13 @@
     sq[1, :, width:] = sums[1]
     edge_swap = swap(1)
     edge_swap.start()
+    ready = []
+    for nodes in (firsts, seconds):
+        pieces = [out_ref[:, n * ne : (n + 1) * ne] for n in nodes]
+        ready.append((nodes, pieces, own_depths(pieces)))
     edge_swap.wait()
-    for part, nodes in enumerate((firsts, seconds)):
-        slots = range(part * 4, part * 4 + 4)
-        radiate(1, slots, nodes, [out_ref[:, n * ne : (n + 1) * ne] for n in nodes])
+    for part, work in enumerate(ready):
+        radiate(1, range(part * 4, part * 4 + 4), *work)
 
     def send(step):
         return pltpu.make_async_remote_copy(

time: 35.1 us -> 35.1 us (level)
  no operation moved by 1% of the time
where the time goes in v5:
time: 35.1 us; the launch traced here: 34.9 us
  Pallas kernels  31.5 us (90%)
  local copies, waits for them, and re-layouts  2.69 us (8%)
  between operations  0.65 us (2%)
    pallas_call x1, Pallas kernels, local(): pl.pallas_call(functools.partial(step_kernel, count, levels), in_specs=[a...  31.5 us
    unnamed x4, local copies, waits for them, and re-layouts  2.69 us

profile of v5, /device:TPU:0, one launch (start us, length us, event | category | flops | bytes accessed | tf_op | source)
XLA Modules:
  0.0 34.9 jit_solution(4974934477102597077)
XLA Ops:
  0.6 31.5 %step.1 = (f32[24,4,2048]{2,1,0:T(4,128)}, f32[1,1024]{1,0:T(1,128)}) custom-call(f32[24,4,2048]{2,1,0:T(4,128)} %state_ref.1, f32[2,128]{1,0:T(2,128)} %metric_ref.1, f32[1,128]{1,0:T(1,128)} %bitcast.11, s32[4,128]{1,0:T(4,128)} %nbr_ref.1, s32[4,128]{1,0:T(4,128)} %side_ref.1, f32[1,2048]{1,0:T(1,128)} %bitcast.8, f32[1,112]{1,0:T(1,128)} %bitcast.12, ...), custom_call_target="tpu_custom_call" | custom-call | tf_op jit(solution)/shard_map/step/pallas_call | solution.py:405
  32.2 0.0 copy-start
  32.2 2.1 %copy.14 = f32[24,4,2048]{2,1,0:T(4,128)} copy(f32[24,4,2048]{2,1,0:T(4,128)} %get-tuple-element.8) | data formatting | bytes 1572864
  34.3 0.0 copy-done
  34.3 0.6 %copy.15 = f32[1024]{0:T(1024)} copy(f32[1024]{0:T(1024)S(1)} %bitcast.10) | data formatting | bytes 8192
Async XLA Ops:
  32.2 2.1 %copy-start = (f32[1,1024]{1,0:T(1,128)S(1)}, f32[1,1024]{1,0:T(1,128)}, u32[]{:S(2)}) copy-start(f32[1,1024]{1,0:T(1,128)} %get-tuple-element.5) | copy-start | bytes 12292
